TPU v7x, 32 devices: a whole 2x2x4 slice. The times are simulated.
32 devices in a mesh: gx: 2 (over y), gy: 4 (over x, core), gz: 4 (over z).
Axes of the slice: x: 2, y: 2, z: 4, core: 2. Of those that a mesh axis runs over, the one named last changes fastest.
Arguments:
- features: float32 [2, 4, 4, 1920, 256], P('gx', 'gy', 'gz'), may hold values from -6 to 6
- slot_voxel: int32 [2, 4, 4, 1920], P('gx', 'gy', 'gz'), may hold values from 0 to 2047, as said below
- block_count: int32 [2, 4, 4], P('gx', 'gy', 'gz'), may hold values from 1 to 15, as said below
- hilbert_dest: int32 [2, 4, 4, 15], P('gx', 'gy', 'gz'), may hold values from -1 to 127, as said below
- transposed_dest: int32 [2, 4, 4, 30], P('gx', 'gy', 'gz'), may hold values from -1 to 127, as said below
- conv_weight: bfloat16 [2, 27, 256, 256], replicated, may hold values from -0.078125 to 0.078125
- qkv_weight: bfloat16 [2, 256, 768], replicated
- proj_weight: bfloat16 [2, 256, 256], replicated, may hold values from -0.375 to 0.375
- up_weight: bfloat16 [2, 256, 1024], replicated, may hold values from -0.375 to 0.375
- down_weight: bfloat16 [2, 1024, 256], replicated, may hold values from -0.1875 to 0.1875
Outputs:
- encoded: float32 [2, 4, 4, 1920, 256], P('gx', 'gy', 'gz')
Inputs may be any that keep to these rules, and one draw needn't show every extreme that they name: `slot_voxel`: within one device the slots carry distinct voxel numbers. `block_count`: along gz, the counts of the devices of one (gx, gy) column sum to 8 times the size of gz; some device holds 15 blocks. `hilbert_dest`: -1 for block j at or past the device's block count, else o * 8 + p with 0 <= p < 8, o numbering the devices of the same gx index as gy index times the size of gz plus gz index. Every such owner and position receives exactly one block; no device sends more than 1 block to one owner, and some device sends 1. `transposed_dest`: -1 for half block h at or past twice the device's block count, else o 2 * 8 + p with 0 <= p < 16, o numbering the devices of the same gy index as gx index times the size of gz plus gz index. Every such owner and position receives exactly one half block; no device sends more than 4 half block to one owner, and some device sends 4.
All inputs are finite; a program needn't handle non-finite values.
Results may differ from a plain program's by a relative error of at most 0.025.
Values may be sent and summed in bfloat16 or wider, within the bound.
No kernel may reach another device: no remote copies, remote signals or barrier semaphores. Data moves between devices by JAX's collectives and lax.ppermute only.
A program may use at most 128 MiB of HBM per device.

v0:
```python
import math

import jax
import jax.numpy as jnp
from jax import lax
from jax.sharding import PartitionSpec as P

HEADS = 16
BLOCK = 128
PATCH_BLOCKS = 8
VX = 16
VY = 16
VZ = 8


EPS = 1e-05


def extended(cells, sides, width):
    for axis, dim in sides:
        count = lax.axis_size(axis)
        ends = count - 1
        head = lax.slice_in_dim(cells, 0, width, axis=dim)
        tail = lax.slice_in_dim(cells, cells.shape[dim] - width, cells.shape[dim], axis=dim)
        cells = jnp.concatenate(
            [
                lax.ppermute(tail, axis, [(i, (i + 1) % count) for i in range(ends)]),
                cells,
                lax.ppermute(head, axis, [((i + 1) % count, i) for i in range(ends)]),
            ],
            axis=dim,
        )
    return cells


def shortened(shard):
    return jax.tree.map(lambda a: a.astype(jnp.bfloat16) if a.dtype == jnp.float32 else a, shard)


def layer_norm(values):
    centred = values - jnp.mean(values, axis=-1, keepdims=True)
    variance = jnp.mean(centred * centred, axis=-1, keepdims=True)
    return centred * lax.rsqrt(variance + EPS)


def attend(patch_rows, qkv_matrix, out_matrix):
    patch_count, patch_len, channels = patch_rows.shape
    head_width = channels // HEADS
    normed = layer_norm(patch_rows).astype(jnp.bfloat16).reshape(-1, channels)
    packed = jnp.dot(normed, qkv_matrix, preferred_element_type=jnp.float32).astype(jnp.bfloat16)
    packed = packed.reshape(patch_count, patch_len, 3, HEADS, head_width)
    stacked = jnp.transpose(packed, (2, 3, 0, 1, 4))

    def one_head(operands):
        query_rows, key_entries, value_entries = operands
        logit_scores = jnp.einsum(
            "pld,pmd->plm", query_rows, key_entries, preferred_element_type=jnp.float32
        ) * (1.0 / math.sqrt(head_width))
        row_max = jnp.max(logit_scores, axis=-1, keepdims=True)
        exp_scores = jnp.exp(logit_scores - row_max)
        attention_weights = (exp_scores / jnp.sum(exp_scores, axis=-1, keepdims=True)).astype(
            jnp.bfloat16
        )
        return jnp.einsum(
            "plm,pmd->pld", attention_weights, value_entries, preferred_element_type=jnp.float32
        ).astype(jnp.bfloat16)

    head_result = lax.map(one_head, (stacked[0], stacked[1], stacked[2]))
    merged = jnp.transpose(head_result, (1, 2, 0, 3)).reshape(-1, channels)
    update = jnp.dot(merged, out_matrix, preferred_element_type=jnp.float32)
    return patch_rows + update.reshape(patch_rows.shape)


def feed_forward(point_rows, up_matrix, down_matrix):
    normed = layer_norm(point_rows).astype(jnp.bfloat16)
    hidden = jax.nn.gelu(
        jnp.dot(normed, up_matrix, preferred_element_type=jnp.float32), approximate=False
    ).astype(jnp.bfloat16)
    return point_rows + jnp.dot(hidden, down_matrix, preferred_element_type=jnp.float32)


def convolve(plain, voxels, live_row, attention_weights):
    slot_count, channels = plain.shape
    cell_count = VX * VY * VZ
    target = jnp.where(live_row, voxels, cell_count)
    placing = (jnp.arange(cell_count, dtype=jnp.int32)[:, None] == target[None, :]).astype(
        jnp.bfloat16
    )
    grid = jnp.dot(placing, plain.astype(jnp.bfloat16), preferred_element_type=jnp.float32).astype(
        jnp.bfloat16
    )
    grid = grid.reshape(VX, VY, VZ, channels)
    padded = extended(grid, (("gx", 0), ("gy", 1), ("gz", 2)), 1)
    running = jnp.zeros((cell_count, channels), jnp.float32)
    for offset in range(27):
        window = padded[
            offset // 9 : offset // 9 + VX,
            offset // 3 % 3 : offset // 3 % 3 + VY,
            offset % 3 : offset % 3 + VZ,
        ]
        running = running + jnp.dot(
            window.reshape(cell_count, channels),
            attention_weights[offset],
            preferred_element_type=jnp.float32,
        )
    return running[jnp.where(live_row, voxels, 0)]


def plan_routes(dest, live, per_owner, owners, capacity):
    item_count = dest.shape[0]
    item_index = jnp.arange(item_count, dtype=jnp.int32)
    owner_index = jnp.where(live, dest // per_owner, -1)
    placement = jnp.where(live, dest % per_owner, -1)
    earlier = (owner_index[:, None] == owner_index[None, :]) & (
        item_index[None, :] < item_index[:, None]
    )
    within = jnp.sum(earlier.astype(jnp.int32), axis=1)
    send_slot = jnp.where(live, owner_index * capacity + within, -1)
    buffer_slots = jnp.arange(owners * capacity, dtype=jnp.int32)
    matches = send_slot[None, :] == buffer_slots[:, None]
    source = jnp.sum(jnp.where(matches, item_index[None, :], 0), axis=1)
    filled = jnp.any(matches, axis=1)
    position = jnp.where(filled, placement[source], -1)
    return (send_slot, source, filled, position)


def arrange(received, position_values, positions):
    position_int = position_values.astype(jnp.int32)
    slot_ids = jnp.arange(position_int.shape[0], dtype=jnp.int32)
    wanted = jnp.arange(positions, dtype=jnp.int32)
    anchor = jnp.sum(
        jnp.where(position_int[None, :] == wanted[:, None], slot_ids[None, :], 0), axis=1
    )
    return (received[anchor], position_int)


def scatter_back(result, position_int):
    return jnp.where((position_int >= 0)[:, None, None], result[jnp.maximum(position_int, 0)], 0.0)


def hilbert_trip(stream, dest, live_block, patch_work):
    slot_count, channels = stream.shape
    slot_blocks = dest.shape[0]
    per_owner = (slot_blocks + 1) // 2
    owners = lax.axis_size("gy") * lax.axis_size("gz")
    capacity = -(-slot_blocks // owners)
    send_slot, source, filled, position = plan_routes(dest, live_block, per_owner, owners, capacity)
    pieces = stream.reshape(slot_blocks, slot_count // slot_blocks, channels)
    outgoing = jnp.where(filled[:, None, None], pieces[source], 0.0)
    received, position_values = (
        lax.all_to_all(outgoing, ("gy", "gz"), split_axis=0, concat_axis=0, tiled=True),
        lax.all_to_all(
            position.astype(jnp.float32), ("gy", "gz"), split_axis=0, concat_axis=0, tiled=True
        ),
    )
    arranged, position_int = arrange(received, position_values, per_owner)
    returned = lax.all_to_all(
        scatter_back(patch_work(arranged), position_int).astype(jnp.bfloat16),
        ("gy", "gz"),
        split_axis=0,
        concat_axis=0,
        tiled=True,
    ).astype(jnp.float32)
    restored = jnp.where(live_block[:, None, None], returned[jnp.maximum(send_slot, 0)], 0.0)
    return restored.reshape(slot_count, channels)


def transposed_trip(stream, dest, live_half, patch_work):
    slot_count, channels = stream.shape
    half_total = dest.shape[0]
    per_owner = half_total // 2 + 1
    across = lax.axis_size("gx")
    down_size = lax.axis_size("gz")
    owners = across * down_size
    capacity = -(-half_total // owners)
    send_slot, source, filled, position = plan_routes(dest, live_half, per_owner, owners, capacity)
    pieces = stream.reshape(half_total, slot_count // half_total, channels)
    outgoing = jnp.where(filled[:, None, None], pieces[source], 0.0)
    position_out = position.astype(jnp.float32)
    received, position_values = (
        lax.all_to_all(
            shortened(outgoing), ("gx", "gz"), split_axis=0, concat_axis=0, tiled=True
        ).astype(outgoing.dtype),
        lax.all_to_all(
            position_out.astype(jnp.bfloat16), ("gx", "gz"), split_axis=0, concat_axis=0, tiled=True
        ).astype(position_out.dtype),
    )
    arranged, position_int = arrange(received, position_values, per_owner)
    answer = scatter_back(patch_work(arranged), position_int)
    returned = lax.all_to_all(
        shortened(answer), ("gx", "gz"), split_axis=0, concat_axis=0, tiled=True
    ).astype(answer.dtype)
    restored = jnp.where(live_half[:, None, None], returned[jnp.maximum(send_slot, 0)], 0.0)
    return restored.reshape(slot_count, channels)


def body(
    features,
    slot_voxel,
    block_count,
    hilbert_dest,
    transposed_dest,
    conv_weight,
    qkv_weight,
    proj_weight,
    up_weight,
    down_weight,
):
    slot_count = features.shape[3]
    channels = features.shape[4]
    slot_blocks = hilbert_dest.shape[3]
    block_rows = slot_count // slot_blocks
    live_count = block_count.reshape(())
    live_block = jnp.arange(slot_blocks, dtype=jnp.int32) < live_count
    live_half = jnp.arange(2 * slot_blocks, dtype=jnp.int32) // 2 < live_count
    live_row = jnp.arange(slot_count, dtype=jnp.int32) // block_rows < live_count
    voxels = slot_voxel.reshape(slot_count)
    stream = features.reshape(slot_count, channels)
    for layer_index in range(2):
        plain = jnp.where(live_row[:, None], stream, 0.0)
        stream = stream + layer_norm(convolve(plain, voxels, live_row, conv_weight[layer_index]))

        def patch_work(arranged, level=layer_index):
            patch_rows = arranged.reshape(-1, PATCH_BLOCKS * BLOCK, channels)
            attended = attend(patch_rows, qkv_weight[level], proj_weight[level]).reshape(
                -1, channels
            )
            attended = feed_forward(attended, up_weight[level], down_weight[level])
            return attended.reshape(arranged.shape)

        if layer_index == 0:
            stream = hilbert_trip(stream, hilbert_dest.reshape(slot_blocks), live_block, patch_work)
        else:
            stream = transposed_trip(
                stream, transposed_dest.reshape(2 * slot_blocks), live_half, patch_work
            )
    encoded = jnp.where(live_row[:, None], stream, 0.0)
    return encoded.reshape(1, 1, 1, slot_count, channels)


def solution(mesh):
    in_specs = (
        P("gx", "gy", "gz", None, None),
        P("gx", "gy", "gz", None),
        P("gx", "gy", "gz"),
        P("gx", "gy", "gz", None),
        P("gx", "gy", "gz", None),
        P(),
        P(),
        P(),
        P(),
        P(),
    )
    out_specs = P("gx", "gy", "gz", None, None)
    return jax.shard_map(body, mesh=mesh, in_specs=in_specs, out_specs=out_specs, check_vma=False)
```

profile of v0, /device:TPU:0, one launch (start us, length us, event | category | flops | bytes accessed | tf_op | source)
XLA Modules:
  0.0 455.5 jit_solution(2583588457454469489)
XLA Ops:
  1.4 4.6 %fusion.58 = bf16[2048,256]{1,0:T(8,128)(2,1)S(1)} fusion(s32[1920]{0:T(1024)S(1)} %broadcast_select_fusion.1, f32[1,1,1,1920,256]{4,3,2,1,0:T(8,128)} %param.14, pred[1920]{0:T(1024)(128)(4,1)S(1)} %fusion.232), kind=kOutput, calls=%fused_computation.147 | convolution fusion | flops 2018213888 | bytes 3024256 | tf_op jit(solution)/shard_map/dot_general | solution.py:89
  6.1 4.9 %collective-permute-start = (bf16[1,16,8,256]{3,2,1,0:T(8,128)(2,1)S(1)}, bf16[1,16,8,256]{3,2,1,0:T(8,128)(2,1)S(1)}, u32[]{:S(2)}, u32[]{:S(2)}) collective-permute-start(bf16[1,16,8,256]{3,2,1,0:T(8,128)(2,1)S(1)} %get-tuple-element.165), channel_id=1, source_target_pairs={{0,16},{1,17},{2,18},{3,19},{4,20},{5,21},{6,22},{7,23},{8,24},{9,... | collective-permute-start | bytes 196616 | tf_op jit(solution)/shard_map/ppermute | solution.py:27
  14.1 5.9 %all-to-all-start.1 = ((f32[16,1,1]{2,1,0:T(1,128)}), f32[16,1,1]{2,1,0:T(1,128)S(1)}, u32[]{:S(2)}, u32[]{:S(2)}) async-start(f32[16,1,1]{2,1,0:T(1,128)} %copy.24), calls=%async_computation.1 | async-start | bytes 16384 | tf_op jit(solution)/shard_map/all_to_all | solution.py:152
  20.2 2.3 collective-permute-start.2
  24.9 1.8 collective-permute-done.3
  27.4 3.4 collective-permute-start.4
  32.4 2.4 fusion.322
  34.7 2.7 fusion.171
  37.4 4.2 collective-permute-done.5
  41.6 2.5 maximum_maximum_fusion
  44.1 6.9 %fusion.318 = (bf16[16,16,8,256]{3,2,1,0:T(8,128)(2,1)}, bf16[16,16,8,256]{3,2,1,0:T(8,128)(2,1)}, bf16[16,16,8,256]{3,2,1,0:T(8,128)(2,1)}, bf16[16,16,8,256]{3...) fusion(bf16[18,18,9,256]{3,2,1,0:T(8,128)(2,1)S(1)} %get-tuple-, ...), kind=kLoop, calls=%fused_computation.540 | loop fusion | bytes 37748736 | tf_op jit(solution)/shard_map/slice | solution.py:96
  89.1 6.2 %gather_fusion.2 = f32[1920,256]{1,0:T(8,128)} fusion(f32[2048,256]{1,0:T(8,128)S(1)} %convolution_add_fusion.24, s32[2048]{0:T(1024)S(1)} %pad_clamp_fusion), kind=kCustom, calls=%fused_computation.2 | custom fusion | bytes 3939840 | tf_op jit(solution)/shard_map/gather | solution.py:106
  95.3 2.0 reduce_sum.198
  97.3 2.2 multiply_reduce_fusion.3
  99.5 3.4 multiply_add_fusion.1
  102.9 2.2 gather_fusion.3
  106.8 4.9 %all-to-all-start.2 = ((f32[16,128,256]{2,1,0:T(8,128)}), f32[16,128,256]{2,1,0:T(8,128)S(1)}, u32[]{:S(2)}, u32[]{:S(2)}) async-start(f32[16,128,256]{2,1,0:T(8,128)} %broadcast_select_fusion), calls=%async_computation.2 | async-start | bytes 4194304 | tf_op jit(solution)/shard_map/all_to_all | solution.py:151
  113.0 48.1 %all-to-all-done.2 = f32[16,128,256]{2,1,0:T(8,128)S(1)} async-done(((f32[16,128,256]{2,1,0:T(8,128)}), f32[16,128,256]{2,1,0:T(8,128)S(1)}, u32[]{:S(2)}, u32[]{:S(2)}) %all-to-all-start.2) | async-done | bytes 2097184 | tf_op jit(solution)/shard_map/all_to_all | solution.py:151
  162.3 1.9 convolution_convert_fusion.1
  164.5 37.9 %while.20 = (s32[]{:T(128)}, bf16[16,1,1024,16]{2,3,1,0:T(8,128)(2,1)S(1)}, bf16[16,1,1024,16]{2,3,1,0:T(8,128)(2,1)S(1)}, bf16[16,1,1024,16]{2,3,1,0:T(8,128)(2...) while((s32[]{:T(128)}, bf16[16,1,1024,16]{2,3,1,0:T(8,128)(2,1)S(1)}, ...), condition=%wide.region_14.15_spmd, body=%wide.region_11.14_spmd.sunk | while | flops 76560384 | bytes 12736581 | solution.py:68
  203.2 11.0 %fusion.71 = bf16[1024,256]{1,0:T(8,128)(2,1)S(1)} fusion(f32[1024,256]{1,0:T(8,128)S(1)} %get-tuple-element.176, bf16[2,1024,256]{2,1,0:T(8,128)(2,1)} %param.23, bf16[2,256,1024]{2,1,0:T(8,128)(2,1)} %param.22, f32[1024]{0:T(1024)S(1)} %add_rsqrt_fusion.3, f32[1024]{0:T(1024)S(1)} %broadcast_multiply_fusion.4), kind=kOutput, calls=%fused_computation.170 | convolution fusion | flops 1143209984 | bytes 3678208 | tf_op jit(solution)/shard_map/dot_general | solution.py:79
  216.2 3.8 all-to-all-start.3
  221.3 25.5 %all-to-all-done.3 = bf16[16,128,256]{2,1,0:T(8,128)(2,1)S(1)} async-done(((bf16[16,128,256]{2,1,0:T(8,128)(2,1)}), bf16[16,128,256]{2,1,0:T(8,128)(2,1)S(1)}, u32[]{:S(2)}, u32[]{:S(2)}) %all-to-all-start.3) | async-done | bytes 1048608 | tf_op jit(solution)/shard_map/all_to_all | solution.py:157
  247.1 1.9 gather_fusion.6
  249.0 2.5 fusion.69
  251.6 3.0 fusion.59
  254.6 4.5 collective-permute-start.6
  261.1 4.2 all-to-all-start
  268.3 3.6 collective-permute-done.9
  274.5 4.1 collective-permute-start.10
  282.2 2.5 collective-permute-done.10
  284.7 4.7 %collective-permute-done.11 = bf16[18,18,1,256]{3,2,1,0:T(2,128)(2,1)S(1)} collective-permute-done((bf16[18,18,1,256]{3,2,1,0:T(2,128)(2,1)S(1)}, bf16[18,18,1,256]{3,2,1,0:T(2,128)(2,1)S(1)}, u32[]{:S(2)}, u32[]{:S(2)}) %collective-permute-start.11) | collective-permute-done | bytes 165920 | tf_op jit(solution)/shard_map/ppermute | solution.py:29
  289.4 2.7 maximum_maximum_fusion.1
  292.1 2.4 fusion.317
  294.6 4.2 fusion.316
  317.1 5.9 %gather_fusion.7 = f32[1920,256]{1,0:T(8,128)} fusion(f32[2048,256]{1,0:T(8,128)S(1)} %convolution_add_fusion, s32[2048]{0:T(1024)S(1)} %pad_clamp_fusion), kind=kCustom, calls=%fused_computation.7 | custom fusion | bytes 3939840 | tf_op jit(solution)/shard_map/gather | solution.py:106
  323.0 2.0 reduce_sum.207
  325.1 2.2 multiply_reduce_fusion.2
  327.4 2.0 multiply_add_fusion
  331.3 4.5 all-to-all-start.4
  336.2 27.3 %all-to-all-done.4 = bf16[32,64,256]{2,1,0:T(8,128)(2,1)S(1)} async-done(((bf16[32,64,256]{2,1,0:T(8,128)(2,1)}), bf16[32,64,256]{2,1,0:T(8,128)(2,1)S(1)}, u32[]{:S(2)}, u32[]{:S(2)}) %all-to-all-start.4) | async-done | bytes 1048608 | tf_op jit(solution)/shard_map/all_to_all | solution.py:181
  365.2 1.9 convolution_convert_fusion
  367.3 37.9 %while.21 = (s32[]{:T(128)}, bf16[16,1,1024,16]{2,3,1,0:T(8,128)(2,1)S(1)}, bf16[16,1,1024,16]{2,3,1,0:T(8,128)(2,1)S(1)}, bf16[16,1,1024,16]{2,3,1,0:T(8,128)(2...) while((s32[]{:T(128)}, bf16[16,1,1024,16]{2,3,1,0:T(8,128)(2,1)S(1)}, ...), condition=%wide.region_25.26_spmd, body=%wide.region_22.25_spmd.sunk | while | flops 76560384 | bytes 12736581 | solution.py:68
  406.1 11.0 %fusion.74 = bf16[1024,256]{1,0:T(8,128)(2,1)S(1)} fusion(f32[1024,256]{1,0:T(8,128)S(1)} %get-tuple-element.178, bf16[2,1024,256]{2,1,0:T(8,128)(2,1)} %param.23, bf16[2,256,1024]{2,1,0:T(8,128)(2,1)} %param.22, f32[1024]{0:T(1024)S(1)} %add_rsqrt_fusion.2, f32[1024]{0:T(1024)S(1)} %broadcast_multiply_fusion.3), kind=kOutput, calls=%fused_computation.171 | convolution fusion | flops 1143209984 | bytes 3678208 | tf_op jit(solution)/shard_map/dot_general | solution.py:79
  418.9 3.6 all-to-all-start.5
  422.7 26.9 %all-to-all-done.5 = bf16[32,64,256]{2,1,0:T(8,128)(2,1)S(1)} async-done(((bf16[32,64,256]{2,1,0:T(8,128)(2,1)}), bf16[32,64,256]{2,1,0:T(8,128)(2,1)S(1)}, u32[]{:S(2)}, u32[]{:S(2)}) %all-to-all-start.5) | async-done | bytes 1048608 | tf_op jit(solution)/shard_map/all_to_all | solution.py:190
  449.9 1.9 gather_fusion.11
  451.8 3.5 select_select_fusion
  (360 shorter events, 166.6 us)
Async XLA Ops:
  1.4 10.9 %copy-start.42 = (s32[1,1,1,15]{3,2,1,0:T(1,128)S(1)}, s32[1,1,1,15]{3,2,1,0:T(1,128)}, u32[]{:S(2)}) copy-start(s32[1,1,1,15]{3,2,1,0:T(1,128)} %param.17) | copy-start | bytes 184
  1.4 18.6 %copy-start.41 = (s32[1,1,1,1920]{3,2,1,0:T(1,128)S(1)}, s32[1,1,1,1920]{3,2,1,0:T(1,128)}, u32[]{:S(2)}) copy-start(s32[1,1,1,1920]{3,2,1,0:T(1,128)} %param.15) | copy-start | bytes 23044
  6.1 14.0 %collective-permute-start = (bf16[1,16,8,256]{3,2,1,0:T(8,128)(2,1)S(1)}, bf16[1,16,8,256]{3,2,1,0:T(8,128)(2,1)S(1)}, u32[]{:S(2)}, u32[]{:S(2)}) collective-permute-start(bf16[1,16,8,256]{3,2,1,0:T(8,128)(2,1)S(1)} %get-tuple-element.165), channel_id=1, source_target_pairs={{0,16},{1,17},{2,18},{3,19},{4,20},{5,21},{6,22},{7,23},{8,24},{9,... | collective-permute-start | bytes 196616 | tf_op jit(solution)/shard_map/ppermute | solution.py:27
  11.0 9.1 %collective-permute-start.1 = (bf16[1,16,8,256]{3,2,1,0:T(8,128)(2,1)S(1)}, bf16[1,16,8,256]{3,2,1,0:T(8,128)(2,1)S(1)}, u32[]{:S(2)}, u32[]{:S(2)}) collective-permute-start(bf16[1,16,8,256]{3,2,1,0:T(8,128)(2,1)S(1)} %get-tuple-element.166), channel_id=1, source_target_pairs={{16,0},{17,1},{18,2},{19,3},{20,4},{21,5},{22,6},{23,7},{24,8},{25... | collective-permute-start | bytes 196616 | tf_op jit(solution)/shard_map/ppermute | solution.py:29
  14.1 92.7 %all-to-all-start.1 = ((f32[16,1,1]{2,1,0:T(1,128)}), f32[16,1,1]{2,1,0:T(1,128)S(1)}, u32[]{:S(2)}, u32[]{:S(2)}) async-start(f32[16,1,1]{2,1,0:T(1,128)} %copy.24), calls=%async_computation.1 | async-start | bytes 16384 | tf_op jit(solution)/shard_map/all_to_all | solution.py:152
  20.2 4.8 %collective-permute-start.2 = (bf16[18,1,8,256]{3,2,1,0:T(8,128)(2,1)S(1)}, bf16[18,1,8,256]{3,2,1,0:T(8,128)(2,1)S(1)}, u32[]{:S(2)}, u32[]{:S(2)}) collective-permute-start(bf16[18,1,8,256]{3,2,1,0:T(8,128)(2,1)S(1)} %get-tuple-element.157), channel_id=1, source_target_pairs={{0,4},{4,8},{8,12},{1,5},{5,9},{9,13},{2,6},{6,10},{10,14},{3,7},{... | collective-permute-start | bytes 221192 | tf_op jit(solution)/shard_map/ppermute | solution.py:27
  22.5 4.3 collective-permute-start.3
  27.4 10.0 %collective-permute-start.4 = (bf16[18,18,1,256]{3,2,1,0:T(2,128)(2,1)S(1)}, bf16[18,18,1,256]{3,2,1,0:T(2,128)(2,1)S(1)}, u32[]{:S(2)}, u32[]{:S(2)}) collective-permute-start(bf16[18,18,1,256]{3,2,1,0:T(2,128)(2,1)S(1)} %get-tuple-element.137), channel_id=1, source_target_pairs={{0,1},{1,2},{2,3},{4,5},{5,6},{6,7},{8,9},{9,10},{10,11},{12,13},{... | collective-permute-start | bytes 497672 | tf_op jit(solution)/shard_map/ppermute | solution.py:27
  30.8 10.8 %collective-permute-start.5 = (bf16[18,18,1,256]{3,2,1,0:T(2,128)(2,1)S(1)}, bf16[18,18,1,256]{3,2,1,0:T(2,128)(2,1)S(1)}, u32[]{:S(2)}, u32[]{:S(2)}) collective-permute-start(bf16[18,18,1,256]{3,2,1,0:T(2,128)(2,1)S(1)} %get-tuple-element.138), channel_id=1, source_target_pairs={{1,0},{2,1},{3,2},{5,4},{6,5},{7,6},{9,8},{10,9},{11,10},{13,12},{... | collective-permute-start | bytes 497672 | tf_op jit(solution)/shard_map/ppermute | solution.py:29
  51.0 1.9 copy-start.2
  51.0 2.2 copy-start.33
  51.0 3.5 copy-start.32
  54.6 1.5 copy-start.31
  56.0 1.5 copy-start.3
  57.5 1.5 copy-start.28
  58.9 1.5 copy-start.12
  60.4 1.5 copy-start.26
  61.8 1.5 copy-start.24
  63.3 1.5 copy-start.9
  64.7 1.5 copy-start.22
  69.0 1.5 copy-start.4
  69.0 3.0 copy-start.18
  70.5 2.8 copy-start.17
  73.3 1.5 copy-start.7
  74.8 1.5 copy-start.15
  76.2 1.5 copy-start.14
  77.7 1.5 copy-start.6
  79.1 1.5 copy-start.13
  80.6 1.5 copy-start.11
  83.4 1.5 copy-start.10
  84.9 1.5 copy-start.5
  95.3 4.2 copy-start.1
  106.8 54.2 %all-to-all-start.2 = ((f32[16,128,256]{2,1,0:T(8,128)}), f32[16,128,256]{2,1,0:T(8,128)S(1)}, u32[]{:S(2)}, u32[]{:S(2)}) async-start(f32[16,128,256]{2,1,0:T(8,128)} %broadcast_select_fusion), calls=%async_computation.2 | async-start | bytes 4194304 | tf_op jit(solution)/shard_map/all_to_all | solution.py:151
  164.4 37.9 %copy-start.40 = (bf16[2,256,256]{2,1,0:T(8,128)(2,1)S(1)}, bf16[2,256,256]{2,1,0:T(8,128)(2,1)}, u32[]{:S(2)}) copy-start(bf16[2,256,256]{2,1,0:T(8,128)(2,1)} %param.21) | copy-start | bytes 786436
  214.2 5.8 %copy-start.43 = (s32[1,1,1,30]{3,2,1,0:T(1,128)S(1)}, s32[1,1,1,30]{3,2,1,0:T(1,128)}, u32[]{:S(2)}) copy-start(s32[1,1,1,30]{3,2,1,0:T(1,128)} %param.18) | copy-start | bytes 364
  216.2 30.7 %all-to-all-start.3 = ((bf16[16,128,256]{2,1,0:T(8,128)(2,1)}), bf16[16,128,256]{2,1,0:T(8,128)(2,1)S(1)}, u32[]{:S(2)}, u32[]{:S(2)}) async-start(bf16[16,128,256]{2,1,0:T(8,128)(2,1)} %select_convert_fusion.2), calls=%async_computation.3 | async-start | bytes 2097152 | tf_op jit(solution)/shard_map/all_to_all | solution.py:157
  254.6 10.9 %collective-permute-start.6 = (bf16[1,16,8,256]{3,2,1,0:T(8,128)(2,1)S(1)}, bf16[1,16,8,256]{3,2,1,0:T(8,128)(2,1)S(1)}, u32[]{:S(2)}, u32[]{:S(2)}) collective-permute-start(bf16[1,16,8,256]{3,2,1,0:T(8,128)(2,1)S(1)} %get-tuple-element.161), channel_id=1, source_target_pairs={{0,16},{1,17},{2,18},{3,19},{4,20},{5,21},{6,22},{7,23},{8,24},{9,... | collective-permute-start | bytes 196616 | tf_op jit(solution)/shard_map/ppermute | solution.py:27
  259.1 6.4 %collective-permute-start.7 = (bf16[1,16,8,256]{3,2,1,0:T(8,128)(2,1)S(1)}, bf16[1,16,8,256]{3,2,1,0:T(8,128)(2,1)S(1)}, u32[]{:S(2)}, u32[]{:S(2)}) collective-permute-start(bf16[1,16,8,256]{3,2,1,0:T(8,128)(2,1)S(1)} %get-tuple-element.162), channel_id=1, source_target_pairs={{16,0},{17,1},{18,2},{19,3},{20,4},{21,5},{22,6},{23,7},{24,8},{25... | collective-permute-start | bytes 196616 | tf_op jit(solution)/shard_map/ppermute | solution.py:29
  261.1 70.2 %all-to-all-start = ((bf16[8,4,1]{1,2,0:T(2,128)(2,1)}), bf16[8,4,1]{1,2,0:T(2,128)(2,1)S(1)}, u32[]{:S(2)}, u32[]{:S(2)}) async-start(bf16[8,4,1]{1,2,0:T(2,128)(2,1)} %convert_element_type.248), calls=%async_computation | async-start | bytes 8192 | tf_op jit(solution)/shard_map/all_to_all | solution.py:184
  265.5 2.8 collective-permute-start.8
  266.8 5.1 %collective-permute-start.9 = (bf16[18,1,8,256]{3,2,1,0:T(8,128)(2,1)S(1)}, bf16[18,1,8,256]{3,2,1,0:T(8,128)(2,1)S(1)}, u32[]{:S(2)}, u32[]{:S(2)}) collective-permute-start(bf16[18,1,8,256]{3,2,1,0:T(8,128)(2,1)S(1)} %get-tuple-element.154), channel_id=1, source_target_pairs={{4,0},{8,4},{12,8},{5,1},{9,5},{13,9},{6,2},{10,6},{14,10},{7,3},{... | collective-permute-start | bytes 221192 | tf_op jit(solution)/shard_map/ppermute | solution.py:29
  272.2 9.6 %slice-start = ((s8[7077888]{0:T(1024)(128)(4,1)}), s8[4194304]{0:T(1024)(128)(4,1)S(1)}, s32[]{:S(2)}) async-start(s8[7077888]{0:T(1024)(128)(4,1)} %bitcast.546), calls=%async_computation.6 | async-start | bytes 8388608
  273.9 7.8 %slice-start.1 = ((s8[7077888]{0:T(1024)(128)(4,1)}), s8[2883584]{0:T(1024)(128)(4,1)S(1)}, s32[]{:S(2)}) async-start(s8[7077888]{0:T(1024)(128)(4,1)} %bitcast.546), calls=%async_computation.7 | async-start | bytes 5767168
  274.5 10.2 %collective-permute-start.10 = (bf16[18,18,1,256]{3,2,1,0:T(2,128)(2,1)S(1)}, bf16[18,18,1,256]{3,2,1,0:T(2,128)(2,1)S(1)}, u32[]{:S(2)}, u32[]{:S(2)}) collective-permute-start(bf16[18,18,1,256]{3,2,1,0:T(2,128)(2,1)S(1)} %get-tuple-element.133), channel_id=1, source_target_pairs={{0,1},{1,2},{2,3},{4,5},{5,6},{6,7},{8,9},{9,10},{10,11},{12,13},{... | collective-permute-start | bytes 497672 | tf_op jit(solution)/shard_map/ppermute | solution.py:27
  278.6 10.8 %collective-permute-start.11 = (bf16[18,18,1,256]{3,2,1,0:T(2,128)(2,1)S(1)}, bf16[18,18,1,256]{3,2,1,0:T(2,128)(2,1)S(1)}, u32[]{:S(2)}, u32[]{:S(2)}) collective-permute-start(bf16[18,18,1,256]{3,2,1,0:T(2,128)(2,1)S(1)} %get-tuple-element.134), channel_id=1, source_target_pairs={{1,0},{2,1},{3,2},{5,4},{6,5},{7,6},{9,8},{10,9},{11,10},{13,12},{... | collective-permute-start | bytes 497672 | tf_op jit(solution)/shard_map/ppermute | solution.py:29
  323.0 4.4 copy-start
  331.3 32.2 %all-to-all-start.4 = ((bf16[32,64,256]{2,1,0:T(8,128)(2,1)}), bf16[32,64,256]{2,1,0:T(8,128)(2,1)S(1)}, u32[]{:S(2)}, u32[]{:S(2)}) async-start(bf16[32,64,256]{2,1,0:T(8,128)(2,1)} %select_convert_fusion.1), calls=%async_computation.4 | async-start | bytes 2097152 | tf_op jit(solution)/shard_map/all_to_all | solution.py:181
  418.9 30.7 %all-to-all-start.5 = ((bf16[32,64,256]{2,1,0:T(8,128)(2,1)}), bf16[32,64,256]{2,1,0:T(8,128)(2,1)S(1)}, u32[]{:S(2)}, u32[]{:S(2)}) async-start(bf16[32,64,256]{2,1,0:T(8,128)(2,1)} %select_convert_fusion), calls=%async_computation.5 | async-start | bytes 2097152 | tf_op jit(solution)/shard_map/all_to_all | solution.py:190
  (16 other events, 20.6 us)
where the time goes:
time: 462 us; the launch traced here: 455 us
  waiting for transfers between devices  145 us (31%)
  matrix products  138 us (30%)
  other arithmetic  62.6 us (14%)
  starting transfers between devices  55.3 us (12%)
  local copies, waits for them, and re-layouts  52 us (11%)
    dot_general x54, matrix products, convolve(): jnp.dot(window.reshape(cell_count, channels), attention_weights[offset],...  51.5 us
    all_to_all x1, waiting for transfers between devices, hilbert_trip(): lax.all_to_all(outgoing, ('gy', 'gz'), split_axis=0, concat_axis=0, tiled...  48.1 us
    dot_general x32, matrix products, one_head(): jnp.einsum('plm,pmd->pld', attention_weights, value_entries, preferred_el...  27.9 us
    all_to_all x1, waiting for transfers between devices, transposed_trip(): lax.all_to_all(shortened(outgoing), ('gx', 'gz'), split_axis=0, concat_ax...  27.3 us
    all_to_all x1, waiting for transfers between devices, transposed_trip(): lax.all_to_all(shortened(answer), ('gx', 'gz'), split_axis=0, concat_axis...  26.9 us
    all_to_all x1, waiting for transfers between devices, hilbert_trip(): lax.all_to_all(scatter_back(patch_work(arranged), position_int).astype(jn...  25.5 us
    dot_general x32, matrix products, one_head(): jnp.einsum('pld,pmd->plm', query_rows, key_entries, preferred_element_typ...  24.3 us
    reduce_sum x32, other arithmetic, one_head(): jnp.sum(exp_scores, axis=-1, keepdims=True)  23.3 us
  transfers between devices with their start and end apart: 18, of which 9 were waited for; matrix products, arithmetic and copies ran while one was open for 26% of the time, Pallas kernels for 0%

commit v1 on v0

v1 whole, which is shorter than its diff:
```python
import functools
import math

import jax
import jax.numpy as jnp
from jax import lax
from jax.experimental import pallas as pl
from jax.experimental.pallas import tpu as pltpu
from jax.sharding import PartitionSpec as P

HEADS = 16
PATCH = 1024
VX = 16
VY = 16
VZ = 8
PX = VX + 2
PZ = 16
CELLS = VX * VY * VZ
PLANE = PX * PZ
EPS = 1e-05
CLIP = 3e38
HELD = 12
F32 = jnp.float32
BF16 = jnp.bfloat16
SMEM = pltpu.MemorySpace.SMEM


def call(kernel, outs, ins, scratch=(), name=None, limit=24, flops=0):
    spaces = {"s": SMEM, "v": pltpu.MemorySpace.VMEM, "h": pltpu.MemorySpace.HBM}

    def spec(where):
        return pl.BlockSpec(memory_space=spaces[where]) if isinstance(where, str) else where

    windowed = any(not isinstance(where, str) for _, where in ins)
    result = pl.pallas_call(
        kernel,
        out_shape=tuple(shape for shape, _ in outs),
        grid=(1,) if windowed else (),
        in_specs=[spec(where) for _, where in ins],
        out_specs=tuple(spec(where) for _, where in outs),
        scratch_shapes=list(scratch),
        name=name,
        cost_estimate=pl.CostEstimate(flops=flops, transcendentals=0, bytes_accessed=1 << 20) if flops else None,
        compiler_params=pltpu.CompilerParams(vmem_limit_bytes=limit * 1024 * 1024),
    )(*(array for array, _ in ins))
    return result if len(outs) > 1 else result[0]


def row_groups(rows):
    return next(g for g in (5, 4, 3, 2, 1) if rows % (g * 128) == 0)


def group_copies(src_ref, dst_ref, sems):
    groups = sems.shape[0]
    size = min(src_ref.shape[0], dst_ref.shape[0]) // groups
    parts = [slice(g * size, (g + 1) * size) for g in range(groups)]
    return parts, [pltpu.make_async_copy(src_ref.at[p], dst_ref.at[p], sems.at[g]) for g, p in enumerate(parts)]


def weight_copies(layer, w_ref, dst_ref, sems):
    return [pltpu.make_async_copy(w_ref.at[layer, pl.ds(9 * da, 9)], dst_ref.at[pl.ds(9 * da, 9)], sems.at[da]) for da in range(3)]


def tap(w_ref, da, db, dc):
    return w_ref[9 * da + 3 * db + dc]


def sds(shape, dtype):
    return jax.ShapeDtypeStruct(shape, dtype)


def layer_norm(values):
    centred = values - jnp.mean(values, axis=-1, keepdims=True)
    variance = jnp.mean(centred * centred, axis=-1, keepdims=True)
    return centred * lax.rsqrt(variance + EPS)


def iota(shape, dim):
    return lax.broadcasted_iota(jnp.int32, shape, dim)


def cell_of(voxel):
    x = voxel // (VY * VZ)
    y = (voxel // VZ) % VY
    z = voxel % VZ
    return (x * VZ + z) * VY + y


def voxel_row(vox_ref):
    return jnp.concatenate([vox_ref[j] for j in range(vox_ref.shape[0])], axis=1)


def onehot(mask):
    return jnp.where(mask, 1.0, 0.0).astype(BF16)


def assign_slots(dest_ref, count_ref, slot_ref, used_ref, owners, capacity, per_owner, units_per_block):
    units = dest_ref.shape[0]

    def clear(o, c):
        used_ref[o] = 0
        return c

    lax.fori_loop(0, owners, clear, 0)

    def step(j, c):
        owner = jnp.maximum(dest_ref[j], 0) // per_owner
        rank = used_ref[owner]
        slot_ref[j] = jnp.minimum(owner * capacity + rank, owners * capacity - 1)
        used_ref[owner] = rank + 1
        return c

    lax.fori_loop(0, jnp.minimum(count_ref[0] * units_per_block, units), step, 0)


def place(rows_ref, ids, flags_ref, own_ref, xmsg_ref, ymsg_ref):
    slots = rows_ref.shape[0]
    tile = 256

    def one(t, c):
        r = iota((tile, slots), 0) + t * tile
        hot = onehot(r == ids)
        own_ref[pl.ds(pl.multiple_of(t * tile, tile), tile), :] = jnp.dot(
            hot, rows_ref[...], preferred_element_type=F32
        ).astype(BF16)
        return c

    lax.fori_loop(0, CELLS // tile, one, 0)
    face_rows = VZ * VY
    low, high = own_ref[0:face_rows], own_ref[CELLS - face_rows : CELLS]
    if xmsg_ref.shape[0] == 1:
        xmsg_ref[0] = jnp.where(flags_ref[1] > 0, high, low)
    else:
        xmsg_ref[0] = low
        xmsg_ref[1] = high
    for face in range(2):
        r = iota((PLANE, 1), 0)
        x = r // PZ - 1
        z = r % PZ - 1
        inside = (x >= 0) & (x < VX) & (z >= 0) & (z < VZ)
        cell = jnp.where(inside, (x * VZ + z) * VY + (VY - 1) * face, -2)
        hot = onehot(cell == ids)
        ymsg_ref[face] = jnp.dot(hot, rows_ref[...], preferred_element_type=F32).astype(BF16)


def place_first_kernel(
    layer, block, flags_ref, count_ref, vox_ref, feat_ref, w_in_ref, own_ref, xmsg_ref, ymsg_ref, w_ref, rows_ref, wsems
):
    slots = feat_ref.shape[0]
    weights = weight_copies(layer, w_in_ref, w_ref, wsems)
    for copy in weights:
        copy.start()
    rows_ref[...] = feat_ref[...].astype(BF16)
    live = iota((1, slots), 1) < count_ref[0] * block
    ids = jnp.where(live, cell_of(voxel_row(vox_ref)), -1)
    place(rows_ref, ids, flags_ref, own_ref, xmsg_ref, ymsg_ref)
    for copy in weights:
        copy.wait()


def restore_unit(u, unit, live_units, slot_ref, first_ref, backs):
    alive = u < live_units
    slot = jnp.where(alive, slot_ref[u], 0)
    part = unit // len(backs)
    for k, back_ref in enumerate(backs):
        rows = pl.ds(pl.multiple_of(u * unit + k * part, part), part)
        total = first_ref[rows, :] + back_ref[slot].astype(F32)
        yield rows, jnp.where(alive, total, 0.0)


def place_next_kernel(
    layer,
    route,
    flags_ref,
    count_ref,
    dest_ref,
    vox_ref,
    first_ref,
    back_a_ref,
    back_b_ref,
    w_in_ref,
    own_ref,
    xmsg_ref,
    ymsg_ref,
    w_ref,
    stream_ref,
    rows_ref,
    first_vmem,
    slot_ref,
    used_ref,
    sems,
    wsems,
):
    owners, capacity, per_owner, units_per_block, unit = route
    slots = first_vmem.shape[0]
    parts, copies = group_copies(first_ref, first_vmem, sems)
    weights = weight_copies(layer, w_in_ref, w_ref, wsems)
    for copy in copies + weights:
        copy.start()
    assign_slots(dest_ref, count_ref, slot_ref, used_ref, owners, capacity, per_owner, units_per_block)
    live_units = count_ref[0] * units_per_block
    per = slots // unit // len(parts)

    def one(u, c):
        for rows, value in restore_unit(u, unit, live_units, slot_ref, first_vmem, (back_a_ref, back_b_ref)):
            stream_ref[rows, :] = value
            rows_ref[rows, :] = value.astype(BF16)
        return c

    for g, copy in enumerate(copies):
        copy.wait()
        lax.fori_loop(g * per, (g + 1) * per, one, 0)
    live = iota((1, slots), 1) < live_units * unit
    ids = jnp.where(live, cell_of(voxel_row(vox_ref)), -1)
    place(rows_ref, ids, flags_ref, own_ref, xmsg_ref, ymsg_ref)
    for copy in weights:
        copy.wait()


def restore_kernel(
    route, count_ref, dest_ref, first_ref, back_a_ref, back_b_ref, out_ref, first_vmem, out_vmem, slot_ref, used_ref, sems, osems
):
    owners, capacity, per_owner, units_per_block, unit = route
    parts, copies = group_copies(first_ref, first_vmem, sems)
    _, sends = group_copies(out_vmem, out_ref, osems)
    for copy in copies:
        copy.start()
    assign_slots(dest_ref, count_ref, slot_ref, used_ref, owners, capacity, per_owner, units_per_block)
    live_units = count_ref[0] * units_per_block
    per = first_vmem.shape[0] // unit // len(parts)

    def one(u, c):
        for rows, value in restore_unit(u, unit, live_units, slot_ref, first_vmem, (back_a_ref, back_b_ref)):
            out_vmem[rows, :] = value
        return c

    for g, copy in enumerate(copies):
        copy.wait()
        lax.fori_loop(g * per, (g + 1) * per, one, 0)
        sends[g].start()
    for send in sends:
        send.wait()


def masked(flag, values):
    return jnp.where(flag > 0, values, jnp.zeros_like(values))


def zface_kernel(after_ref, flags_ref, bottom_ref, top_ref, lo_ref, hi_ref, out_lo_ref, out_hi_ref):
    for out_ref, z, face_ref in ((out_lo_ref, 0, bottom_ref), (out_hi_ref, VZ - 1, top_ref)):
        out_ref[0] = masked(flags_ref[0], lo_ref[z])
        out_ref[PX - 1] = masked(flags_ref[1], hi_ref[z])
        out_ref[1 : 1 + VX] = face_ref[...]


def yface_kernel(after_ref, flags_ref, ymsg_ref, xlo_ref, xhi_ref, zlo_ref, zhi_ref, out_lo_ref, out_hi_ref, src_ref):
    nx = VZ * VY
    nz = PX * VY
    src_ref[...] = jnp.zeros_like(src_ref)
    src_ref[0:nx] = masked(flags_ref[0], xlo_ref[...].reshape(nx, -1))
    src_ref[nx : 2 * nx] = masked(flags_ref[1], xhi_ref[...].reshape(nx, -1))
    src_ref[2 * nx : 2 * nx + nz] = zlo_ref[...].reshape(nz, -1)
    src_ref[2 * nx + nz : 2 * nx + 2 * nz] = zhi_ref[...].reshape(nz, -1)
    r = iota((PLANE, 1), 0)
    x = r // PZ
    z = r % PZ
    inner = (z >= 1) & (z <= VZ)
    for out_ref, face in ((out_lo_ref, 0), (out_hi_ref, 1)):
        y = (VY - 1) * face
        want = jnp.where(inner & (x == 0), (z - 1) * VY + y, -1)
        want = jnp.where(inner & (x == PX - 1), nx + (z - 1) * VY + y, want)
        want = jnp.where(z == 0, 2 * nx + x * VY + y, want)
        want = jnp.where(z == VZ + 1, 2 * nx + nz + x * VY + y, want)
        hot = onehot(iota((PLANE, src_ref.shape[0]), 1) == want)
        extra = jnp.dot(hot, src_ref[...], preferred_element_type=F32)
        out_ref[...] = (ymsg_ref[face].astype(F32) + extra).astype(BF16)


def conv_tiles(w_ref, out_ref, pad_ref, start, stride, count, planes):
    channels = pad_ref.shape[-1]
    rows = planes * VZ * VY

    def one(t, c):
        x0 = start + t * stride
        parts = []
        for da in range(3):
            for dc in range(3):
                window = pad_ref[pl.ds(x0 + da, planes), dc : dc + VZ]
                parts.append(window.reshape(rows, channels))
        lhs = jnp.concatenate(parts, axis=1)
        accs = []
        for db in range(3):
            rhs = jnp.concatenate([tap(w_ref, da, db, dc) for da in range(3) for dc in range(3)], axis=0)
            accs.append(jnp.dot(lhs, rhs, preferred_element_type=F32).reshape(planes * VZ, VY, channels))
        out_ref[pl.ds(pl.multiple_of(t * rows, rows), rows), :] = shift_sum(accs).reshape(rows, channels).astype(BF16)
        return c

    lax.fori_loop(0, count, one, 0)


def shift_sum(accs):
    y = iota(accs[0].shape, 1)
    low = jnp.where(y == 0, 0.0, pltpu.roll(accs[0], 1, 1))
    high = jnp.where(y == VY - 1, 0.0, pltpu.roll(accs[2], VY - 1, 1))
    return low + accs[1] + high


def clear_z(pad_ref, x):
    edge = jnp.zeros(pad_ref.shape[2:], BF16)
    pad_ref[x, 0] = edge
    pad_ref[x, VZ + 1] = edge


def conv_middle_kernel(planes, own_ref, w_ref, out_ref, pad_ref):
    for x in range(planes - 1, VX - planes + 1):
        clear_z(pad_ref, x + 1)
        pad_ref[x + 1, 1 : 1 + VZ] = own_ref[x]
    conv_tiles(w_ref, out_ref, pad_ref, planes, planes, VX // planes - 2, planes)


def conv_ends_kernel(planes, flags_ref, own_ref, xlo_ref, xhi_ref, w_ref, out_ref, pad_ref):
    for x in list(range(planes + 1)) + list(range(VX - planes - 1, VX)):
        clear_z(pad_ref, x + 1)
        pad_ref[x + 1, 1 : 1 + VZ] = own_ref[x]
    for x, halo_ref, k in ((0, xlo_ref, 0), (PX - 1, xhi_ref, 1)):
        clear_z(pad_ref, x)
        pad_ref[x, 1 : 1 + VZ] = masked(flags_ref[k], halo_ref[...])
    conv_tiles(w_ref, out_ref, pad_ref, 0, VX - planes, 2, planes)


def conv_z_kernel(zlo_ref, zhi_ref, w_ref, out_ref):
    channels = zlo_ref.shape[-1]
    for face, halo_ref in ((0, zlo_ref), (1, zhi_ref)):
        lhs = jnp.concatenate([halo_ref[da : da + VX].reshape(VX * VY, channels) for da in range(3)], axis=1)
        accs = []
        for db in range(3):
            rhs = jnp.concatenate([tap(w_ref, da, db, 2 * face) for da in range(3)], axis=0)
            accs.append(jnp.dot(lhs, rhs, preferred_element_type=F32).reshape(VX, VY, channels))
        out_ref[face] = shift_sum(accs)


def conv_finish_kernel(
    planes,
    route,
    count_ref,
    dest_ref,
    vox_ref,
    middle_ref,
    ends_ref,
    zc_ref,
    lo_ref,
    hi_ref,
    w_ref,
    stream_ref,
    first_ref,
    send_ref,
    table_ref,
    first_vmem,
    slot_ref,
    used_ref,
    fsems,
):
    owners, capacity, per_owner, units_per_block, unit = route
    channels = middle_ref.shape[-1]
    assign_slots(dest_ref, count_ref, slot_ref, used_ref, owners, capacity, per_owner, units_per_block)
    for s in range(owners * capacity):
        send_ref[s, 0:16] = jnp.full((16, channels), jnp.inf, BF16)
    per_x = VZ * VY
    edge = planes * per_x
    table_ref[0:edge] = ends_ref[0:edge]
    table_ref[edge : CELLS - edge] = middle_ref[...]
    table_ref[CELLS - edge : CELLS] = ends_ref[edge:]
    for face, z in ((0, 0), (1, VZ - 1)):
        for x in range(VX):
            rows = slice(x * per_x + z * VY, x * per_x + (z + 1) * VY)
            table_ref[rows] = (table_ref[rows].astype(F32) + zc_ref[face, x]).astype(BF16)
    plane_rows = VX * PZ
    for face, plane_ref in ((0, lo_ref), (1, hi_ref)):
        plane = plane_ref[...].reshape(PX, PZ, channels)
        wide = plane.astype(F32)
        shifted = [plane] + [pltpu.roll(wide, PZ - dc, 1).astype(BF16) for dc in (1, 2)]
        parts = [shifted[dc][da : da + VX].reshape(plane_rows, channels) for da in range(3) for dc in range(3)]
        rhs = jnp.concatenate([tap(w_ref, da, 2 * face, dc) for da in range(3) for dc in range(3)], axis=0)
        out = jnp.dot(jnp.concatenate(parts, axis=1), rhs, preferred_element_type=F32)
        table_ref[CELLS + face * plane_rows : CELLS + (face + 1) * plane_rows] = out.astype(BF16)
    blocks, _, block = vox_ref.shape
    group = next(g for g in (3, 2, 1) if blocks % g == 0)
    live = count_ref[0]

    def hot_rows(j):
        v = vox_ref[j]
        vt = jnp.transpose(jnp.broadcast_to(v.astype(F32), (block, block))).astype(jnp.int32)
        x = vt // (VY * VZ)
        y = (vt // VZ) % VY
        z = vt % VZ
        main = (x * VZ + z) * VY + y
        lo = jnp.where(y == 0, CELLS + x * PZ + z, -1)
        hi = jnp.where(y == VY - 1, CELLS + plane_rows + x * PZ + z, -1)
        lane = iota((block, block), 1)
        pieces = []
        for k in range((CELLS + 2 * plane_rows) // block):
            ids = main if k * block < CELLS else (lo if k * block < CELLS + plane_rows else hi)
            pieces.append(onehot(ids == lane + k * block))
        return jnp.concatenate(pieces, axis=1)

    def one(g, c):
        hot = jnp.concatenate([hot_rows(g * group + i) for i in range(group)], axis=0)
        gathered = jnp.dot(hot, table_ref[...], preferred_element_type=F32)
        rows = pl.ds(pl.multiple_of(g * group * block, group * block), group * block)
        first = stream_ref[rows, :] + layer_norm(gathered)
        first_vmem[rows, :] = first
        pltpu.make_async_copy(first_vmem.at[rows], first_ref.at[rows], fsems.at[g]).start()
        packed = jnp.clip(first, -CLIP, CLIP).astype(BF16)
        for i in range(group):
            j = g * group + i

            @pl.when(j < live)
            def _():
                for k in range(units_per_block):
                    low = i * block + k * unit
                    send_ref[slot_ref[j * units_per_block + k]] = packed[low : low + unit]

        return c

    lax.fori_loop(0, blocks // group, one, 0)
    for g in range(blocks // group):
        rows = slice(g * group * block, (g + 1) * group * block)
        pltpu.make_async_copy(first_vmem.at[rows], first_ref.at[rows], fsems.at[g]).wait()


def attend_and_feed(x_ref, q_ref, kt_ref, va_ref, vb_ref, proj_ref, up_ref, down_ref, heads_ref, s0_ref, s1_ref, delta_ref):
    tile, channels = q_ref.shape
    half = channels // 2
    width = channels // HEADS
    scale = math.log2(math.e) / math.sqrt(width)
    group = iota((tile, half), 1) // width

    def score(h, side):
        cols = slice(side * half, (side + 1) * half)
        q = jnp.where(group == h, q_ref[:, cols].astype(F32), 0.0).astype(BF16)
        return jnp.dot(q, kt_ref[cols, :], preferred_element_type=F32)

    def combine(h, side, scores):
        cols = slice(side * half, (side + 1) * half)
        v_ref = (va_ref, vb_ref)[side]
        top = jnp.max(scores, axis=-1, keepdims=True)
        probs = jnp.exp2(((scores - top) * scale).astype(BF16))
        res = jnp.dot(probs, v_ref[...], preferred_element_type=F32)
        heads_ref[:, cols] = jnp.where(group == h, res[:, :half] / res[:, half:], heads_ref[:, cols])

    s0_ref[...] = score(0, 0)

    def head(h, c):
        s1_ref[...] = score(h, 1)
        combine(h, 0, s0_ref[...])
        s0_ref[...] = score(h + 1, 0)
        combine(h, 1, s1_ref[...])
        return c

    lax.fori_loop(0, half // width, head, 0)
    x = x_ref[0:tile, :].astype(F32)
    update = jnp.dot(heads_ref[...].astype(BF16), proj_ref[...], preferred_element_type=F32)
    normed = layer_norm(x + update).astype(BF16)
    hidden = jnp.dot(normed, up_ref[...], preferred_element_type=F32)
    hidden = (0.5 * hidden * (1.0 + lax.erf(hidden * (1.0 / math.sqrt(2.0))))).astype(BF16)
    delta_ref[...] = (update + jnp.dot(hidden, down_ref[...], preferred_element_type=F32)).astype(BF16)


def with_ones(v_ref, va_ref, vb_ref):
    rows, channels = v_ref.shape
    half = channels // 2
    ones = jnp.ones((rows, half), BF16)
    for side, ref in ((0, va_ref), (1, vb_ref)):
        ref[:, :half] = v_ref[:, side * half : (side + 1) * half]
        ref[:, half:] = ones


def answer_copies(pos_ref, delta_ref, out_ref, sems):
    slots, part, _ = out_ref.shape
    copies = []
    for s in range(slots):
        rows = pl.ds(pl.multiple_of(pos_ref[s] * part, part), part)
        copies.append(pltpu.make_async_copy(delta_ref.at[rows], out_ref.at[s], sems.at[s]))
        copies[-1].start()
    return copies


def owner_a_kernel(
    layer,
    recv_in_ref,
    qkv_in_ref,
    proj_in_ref,
    up_in_ref,
    down_in_ref,
    out_ref,
    xb_out_ref,
    qb_out_ref,
    kt_out_ref,
    v_out_ref,
    pos_ref,
    xa_ref,
    xb_ref,
    qa_ref,
    qb_ref,
    kt_ref,
    v_ref,
    va_ref,
    vb_ref,
    heads_ref,
    delta_ref,
    s0_ref,
    s1_ref,
    sems,
    osems,
    recv_ref,
    proj_ref,
    up_ref,
    down_ref,
    wsems,
    qkv_ref,
):
    pairs = ((qkv_in_ref, qkv_ref), (proj_in_ref, proj_ref), (up_in_ref, up_ref), (down_in_ref, down_ref))
    weights = [pltpu.make_async_copy(src.at[layer], dst, wsems.at[k]) for k, (src, dst) in enumerate(pairs)]
    arrival = pltpu.make_async_copy(recv_in_ref, recv_ref, osems.at[0])
    arrival.start()
    for copy in weights:
        copy.start()
    slots, unit, channels = recv_ref.shape
    part = unit // 2
    units = PATCH // unit
    tile = PATCH // 2
    pos = jnp.int32(0)
    arrival.wait()
    for s in range(slots):
        mark = jnp.max(recv_ref[s, 0:16, 0:128].astype(F32))
        pos_ref[s] = jnp.minimum(pos, units - 1)
        rows = pl.ds(pl.multiple_of(pos * part, part), part)
        xa_ref[rows, :] = recv_ref[s, :part]
        xb_ref[rows, :] = recv_ref[s, part:]
        pos = jnp.minimum(pos + jnp.where(mark > CLIP * 1.1, 0, 1), units)
    step = 256
    weights[0].wait()
    for c, (src_ref, dst_ref) in enumerate(((xa_ref, qa_ref), (xb_ref, qb_ref))):
        for t in range(tile // step):
            rows = slice(t * step, (t + 1) * step)
            both = slice(c * tile + t * step, c * tile + (t + 1) * step)
            normed = layer_norm(src_ref[rows, :].astype(F32)).astype(BF16)
            packed = jnp.dot(normed, qkv_ref[...], preferred_element_type=F32)
            dst_ref[rows, :] = packed[:, :channels].astype(BF16)
            kt_ref[:, both] = jnp.transpose(packed[:, channels : 2 * channels]).astype(BF16)
            v_ref[both, :] = packed[:, 2 * channels :].astype(BF16)
    pairs = ((xb_ref.at[0:tile], xb_out_ref), (qb_ref, qb_out_ref), (kt_ref, kt_out_ref), (v_ref, v_out_ref))
    handed = [pltpu.make_async_copy(src, dst, sems.at[k]) for k, (src, dst) in enumerate(pairs)]
    for copy in handed:
        copy.start()
    with_ones(v_ref, va_ref, vb_ref)
    for copy in weights[1:]:
        copy.wait()
    attend_and_feed(
        xa_ref, qa_ref, kt_ref, va_ref, vb_ref, proj_ref, up_ref, down_ref, heads_ref, s0_ref, s1_ref, delta_ref
    )
    for copy in handed + answer_copies(pos_ref, delta_ref, out_ref, osems):
        copy.wait()


def owner_b_kernel(
    layer,
    pos_ref,
    x_in_ref,
    q_in_ref,
    kt_in_ref,
    v_in_ref,
    proj_in_ref,
    up_in_ref,
    down_in_ref,
    out_ref,
    x_ref,
    q_ref,
    kt_ref,
    v_ref,
    va_ref,
    vb_ref,
    heads_ref,
    delta_ref,
    s0_ref,
    s1_ref,
    sems,
    osems,
    proj_ref,
    up_ref,
    down_ref,
    wsems,
):
    pairs = ((proj_in_ref, proj_ref), (up_in_ref, up_ref), (down_in_ref, down_ref))
    weights = [pltpu.make_async_copy(src.at[layer], dst, wsems.at[k]) for k, (src, dst) in enumerate(pairs)]
    pairs = ((q_in_ref, q_ref), (kt_in_ref, kt_ref), (v_in_ref, v_ref), (x_in_ref, x_ref))
    copies = [pltpu.make_async_copy(src, dst, sems.at[k]) for k, (src, dst) in enumerate(pairs)]
    for copy in copies + weights:
        copy.start()
    for copy in copies + weights:
        copy.wait()
    with_ones(v_ref, va_ref, vb_ref)
    attend_and_feed(x_ref, q_ref, kt_ref, va_ref, vb_ref, proj_ref, up_ref, down_ref, heads_ref, s0_ref, s1_ref, delta_ref)
    for copy in answer_copies(pos_ref, delta_ref, out_ref, osems):
        copy.wait()


def owner_work(received, layer, qkv_weight, proj_weight, up_weight, down_weight):
    slots, unit, channels = received.shape
    tile = PATCH // 2
    part = unit // 2
    arrays = (qkv_weight, proj_weight, up_weight, down_weight)
    weights = [(w, "h") for w in arrays]
    held_weights = [pltpu.VMEM(w.shape[1:], BF16) for w in arrays]
    half = pltpu.VMEM((tile, channels), BF16)
    whole = pltpu.VMEM((PATCH, channels), BF16)
    across = pltpu.VMEM((channels, PATCH), BF16)
    held = pltpu.VMEM((tile + part, channels), BF16)
    scores = pltpu.VMEM((tile, PATCH), F32)
    tail = [across, whole, whole, whole, pltpu.VMEM((tile, channels), F32), half, scores, scores]
    tail += [pltpu.SemaphoreType.DMA((4,)), pltpu.SemaphoreType.DMA((slots,))]
    answer = (sds((slots, part, channels), BF16), "h")
    rows = (sds((tile, channels), BF16), "h")
    out_a, xb, qb, kt, v, pos = call(
        functools.partial(owner_a_kernel, layer),
        [answer, rows, rows, (sds((channels, PATCH), BF16), "h"), (sds((PATCH, channels), BF16), "h")]
        + [(sds((slots,), jnp.int32), "s")],
        [(received, "h")] + weights,
        [held, held, half, half]
        + tail
        + [pltpu.VMEM(received.shape, BF16)]
        + held_weights[1:]
        + [pltpu.SemaphoreType.DMA((4,)), held_weights[0]],
        "owner_a",
        61,
        1 << 33,
    )
    out_b = call(
        functools.partial(owner_b_kernel, layer),
        [answer],
        [(pos, "s"), (xb, "h"), (qb, "h"), (kt, "h"), (v, "h")] + weights[1:],
        [half, half] + tail + held_weights[1:] + [pltpu.SemaphoreType.DMA((3,))],
        "owner_b",
        61,
        1 << 33,
    )
    return out_a, out_b


def up_down(axis, low_face, high_face):
    count = lax.axis_size(axis)
    ends = count - 1
    from_low = lax.ppermute(high_face, axis, [(i, (i + 1) % count) for i in range(ends)])
    from_high = lax.ppermute(low_face, axis, [((i + 1) % count, i) for i in range(ends)])
    return from_low, from_high


def exchange_x(faces):
    if faces.shape[0] == 1:
        got = lax.ppermute(faces, "gx", [(0, 1), (1, 0)]).reshape(faces.shape[1:])
        return got, got
    return up_down("gx", faces[0], faces[1])


def body(
    features,
    slot_voxel,
    block_count,
    hilbert_dest,
    transposed_dest,
    conv_weight,
    qkv_weight,
    proj_weight,
    up_weight,
    down_weight,
):
    slot_count = features.shape[3]
    channels = features.shape[4]
    blocks = hilbert_dest.shape[3]
    halves = transposed_dest.shape[3]
    block = slot_count // blocks
    patch_blocks = PATCH // block
    count = block_count.reshape(1)
    vox_block = slot_voxel.reshape(blocks, 1, block)
    stream = features.reshape(slot_count, channels)
    dests = (hilbert_dest.reshape(blocks), transposed_dest.reshape(halves))
    axes = (("gy", "gz"), ("gx", "gz"))
    routes = []
    for layer, dest in enumerate(dests):
        owners = lax.axis_size(axes[layer][0]) * lax.axis_size(axes[layer][1])
        per_block = dest.shape[0] // blocks
        routes.append((owners, -(-dest.shape[0] // owners), patch_blocks * per_block, per_block, block // per_block))
    planes = 4
    if lax.axis_size("gx") == 2:
        index = lax.axis_index("gx")
        flags = jnp.stack([index == 1, index == 0]).astype(jnp.int32)
    else:
        flags = jnp.ones((2,), jnp.int32)
    faces_sent = 1 if lax.axis_size("gx") == 2 else 2
    placed = [(sds((CELLS, channels), BF16), "v"), (sds((faces_sent, VZ * VY, channels), BF16), "v")]
    placed += [(sds((2, PLANE, channels), BF16), "v")]
    placed += [(sds(conv_weight.shape[1:], BF16), "v")]
    weight_sems = pltpu.SemaphoreType.DMA((3,))
    rows_scratch = pltpu.VMEM((slot_count, channels), BF16)
    stream_scratch = pltpu.VMEM((slot_count, channels), F32)
    row_sems = pltpu.SemaphoreType.DMA((row_groups(slot_count),))
    pad_scratch = pltpu.VMEM((PX, VZ + 2, VY, channels), BF16)
    half_conv = CELLS // 2 * 27 * channels * channels * 2

    def route_scratch(layer):
        return [pltpu.SMEM((dests[layer].shape[0],), jnp.int32), pltpu.SMEM((routes[layer][0],), jnp.int32)]

    first = backs = None
    for layer in range(2):
        route = routes[layer]
        owners, capacity, per_owner, per_block, unit = route
        if layer == 0:
            own, xmsg, ymsg, weights = call(
                functools.partial(place_first_kernel, layer, block),
                placed,
                [(flags, "s"), (count, "s"), (vox_block, "v"), (stream, "v"), (conv_weight, "h")],
                [rows_scratch, weight_sems],
                "place0",
                44,
            )
        else:
            own, xmsg, ymsg, weights, stream = call(
                functools.partial(place_next_kernel, layer, routes[layer - 1]),
                placed + [(sds((slot_count, channels), F32), "v")],
                [(flags, "s"), (count, "s"), (dests[layer - 1], "s"), (vox_block, "v"), (first, "h")]
                + [(b, "v") for b in backs]
                + [(conv_weight, "h")],
                [rows_scratch, stream_scratch] + route_scratch(layer - 1) + [row_sems, weight_sems],
                "place1",
                44,
            )
        own = own.reshape(VX, VZ, VY, channels)
        xlo, xhi = exchange_x(xmsg.reshape(-1, VZ, VY, channels))
        middle = call(
            functools.partial(conv_middle_kernel, planes),
            [(sds((CELLS - 2 * planes * VZ * VY, channels), BF16), "v")],
            [(own, "v"), (weights, "v")],
            [pad_scratch],
            "conv_middle",
            24,
            half_conv,
        )
        zshape = (sds((PX, VY, channels), BF16), "v")
        faces = [
            (own, pl.BlockSpec((VX, None, VY, channels), lambda i, z=z: (0, z, 0, 0), pipeline_mode=pl.Buffered(1)))
            for z in (0, VZ - 1)
        ]
        zlow, zhigh = call(
            zface_kernel, [zshape, zshape], [(middle, "h"), (flags, "s")] + faces + [(xlo, "v"), (xhi, "v")], (), "zface", 8
        )
        zlo, zhi = up_down("gz", zlow, zhigh)
        ends = call(
            functools.partial(conv_ends_kernel, planes),
            [(sds((2 * planes * VZ * VY, channels), BF16), "v")],
            [(flags, "s"), (own, "v"), (xlo, "v"), (xhi, "v"), (weights, "v")],
            [pad_scratch],
            "conv_ends",
            24,
            half_conv,
        )
        yshape = (sds((PLANE, channels), BF16), "v")
        ylow, yhigh = call(
            yface_kernel,
            [yshape, yshape],
            [(ends, "h"), (flags, "s"), (ymsg, "v"), (xlo, "v"), (xhi, "v"), (zlo, "v"), (zhi, "v")],
            [pltpu.VMEM((896, channels), BF16)],
            "yface",
            8,
        )
        ylo, yhi = up_down("gy", ylow, yhigh)
        zc = call(
            conv_z_kernel,
            [(sds((2, VX, VY, channels), F32), "v")],
            [(zlo, "v"), (zhi, "v"), (weights, "v")],
            [],
            "conv_z",
            24,
            half_conv // 4,
        )
        slots = owners * capacity
        groups = blocks // next(g for g in (3, 2, 1) if blocks % g == 0)
        first, send = call(
            functools.partial(conv_finish_kernel, planes, route),
            [(sds((HELD * slot_count, channels), F32), "h"), (sds((slots, unit, channels), BF16), "v")],
            [(count, "s"), (dests[layer], "s"), (vox_block, "v"), (middle, "v"), (ends, "v"), (zc, "v")]
            + [(ylo, "v"), (yhi, "v"), (weights, "v"), (stream, "v")],
            [
                pltpu.VMEM((CELLS + 2 * VX * PZ, channels), BF16),
                stream_scratch,
            ]
            + route_scratch(layer)
            + [pltpu.SemaphoreType.DMA((groups,))],
            "conv_finish",
            24,
        )
        received = lax.all_to_all(send, axes[layer], split_axis=0, concat_axis=0, tiled=True)
        answers = owner_work(received, layer, qkv_weight, proj_weight, up_weight, down_weight)
        backs = [lax.all_to_all(a, axes[layer], split_axis=0, concat_axis=0, tiled=True) for a in answers]
    encoded = call(
        functools.partial(restore_kernel, routes[1]),
        [(sds((slot_count, channels), F32), "h")],
        [(count, "s"), (dests[1], "s"), (first, "h")] + [(b, "v") for b in backs],
        [stream_scratch, stream_scratch] + route_scratch(1) + [row_sems, row_sems],
        "restore",
        60,
    )
    return encoded.reshape(1, 1, 1, slot_count, channels)


def solution(mesh):
    in_specs = (
        P("gx", "gy", "gz", None, None),
        P("gx", "gy", "gz", None),
        P("gx", "gy", "gz"),
        P("gx", "gy", "gz", None),
        P("gx", "gy", "gz", None),
        P(),
        P(),
        P(),
        P(),
        P(),
    )
    out_specs = P("gx", "gy", "gz", None, None)
    return jax.shard_map(body, mesh=mesh, in_specs=in_specs, out_specs=out_specs, check_vma=False)
```

time: 462 us -> 271 us (0.59); the launches traced: 455 us -> 270 us
  matrix products: 138 us -> 0 us
  waiting for transfers between devices: 145 us -> 7.99 us
  Pallas kernels: 0 us -> 124 us
  blocking collectives: 0 us -> 110 us
  other arithmetic: 62.6 us -> 0.08 us
  local copies, waits for them, and re-layouts: 52 us -> 2.26 us
  starting transfers between devices: 55.3 us -> 24.1 us
    dot_general x126 -> x0, matrix products: 138 us -> none  [the longest x54 51.5 us: convolve(): jnp.dot(window.reshape(cell_count, channels), attention_weights[offset],...]
    all_to_all x6 -> x2, waiting for transfers between devices: 128 us -> 0.01 us  [body(): lax.all_to_all(a, axes[layer], split_axis=0, concat_axis=0, tiled=True)]
    pallas_call x0 -> x19, Pallas kernels: none -> 124 us  [call(): pl.pallas_call(kernel, out_shape=tuple((shape for shape, _ in outs)), gri...]
    all_to_all x0 -> x4, blocking collectives: none -> 110 us  [the longest x2 66.1 us: body(): lax.all_to_all(send, axes[layer], split_axis=0, concat_axis=0, tiled=True)]
    reduce_sum x48 -> x0, other arithmetic: 34.4 us -> none  [the longest x32 23.3 us: one_head(): jnp.sum(exp_scores, axis=-1, keepdims=True)]
    gather x12 -> x0, local copies, waits for them, and re-layouts: 22.7 us -> none  [the longest x2 12.1 us: convolve(): return running[jnp.where(live_row, voxels, 0)]]
    all_to_all x6 -> x2, starting transfers between devices: 27 us -> 7.27 us  [body(): lax.all_to_all(a, axes[layer], split_axis=0, concat_axis=0, tiled=True)]
    slice x8 -> x0, local copies, waits for them, and re-layouts: 19.5 us -> none  [the longest x6 19.4 us: convolve(): padded[offset // 9:offset // 9 + VX, offset // 3 % 3:offset // 3 % 3 + VY...]
  transfers between devices with their start and end apart: 18 -> 12, of which waited for: 9 -> 4; matrix products, arithmetic and copies ran while one was open for 26% -> 0% of each run, Pallas kernels for 0% -> 19%
where the time goes in v1:
time: 271 us; the launch traced here: 270 us
  Pallas kernels  124 us (46%)
  blocking collectives  110 us (41%)
  starting transfers between devices  24.1 us (9%)
  waiting for transfers between devices  7.99 us (3%)
    pallas_call x19, Pallas kernels, call(): pl.pallas_call(kernel, out_shape=tuple((shape for shape, _ in outs)), gri...  124 us
    all_to_all x2, blocking collectives, body(): lax.all_to_all(send, axes[layer], split_axis=0, concat_axis=0, tiled=True)  66.1 us
    all_to_all x2, blocking collectives, body(): lax.all_to_all(a, axes[layer], split_axis=0, concat_axis=0, tiled=True)  44.2 us
    ppermute x4, waiting for transfers between devices, up_down(): lax.ppermute(low_face, axis, [((i + 1) % count, i) for i in range(ends)])  7.96 us
    ppermute x4, starting transfers between devices, up_down(): lax.ppermute(high_face, axis, [(i, (i + 1) % count) for i in range(ends)])  7.88 us
    all_to_all x2, starting transfers between devices, body(): lax.all_to_all(a, axes[layer], split_axis=0, concat_axis=0, tiled=True)  7.27 us
  transfers between devices with their start and end apart: 12, of which 4 were waited for; matrix products, arithmetic and copies ran while one was open for 0% of the time, Pallas kernels for 19%

profile of v1, /device:TPU:0, one launch (start us, length us, event | category | flops | bytes accessed | tf_op | source)
XLA Modules:
  0.0 269.7 jit_solution(1369675521717354536)
XLA Ops:
  0.7 0.1 add_convert_fusion.flags_ref
  0.7 1.5 copy-done
  2.3 0.7 copy-done.1
  3.0 5.1 %place0.1 = (bf16[2048,256]{1,0:T(8,128)(2,1)S(1)}, bf16[1,128,256]{2,1,0:T(8,128)(2,1)S(1)}, bf16[2,288,256]{2,1,0:T(8,128)(2,1)S(1)}, bf16[27,256,256]{2,1,0:T(8,128)(2,1)S(1)}) custom-call(s32[2]{0:T(128)S(1)} %add_convert_fusion.flags_ref, s32[1]{0:T(128)} %bitcast.14.count_ref, s32[15,1,128]{2,1,0:T(1,128)S(1)} %bitcast.41, f32[1920,256]{1,0:T(8,128)S(1)} %bitcast.19, ...), custom_call_target="tpu_custom_call" | custom-call | tf_op jit(solution)/shard_map/place0/pallas_call | solution.py:35
  8.1 3.1 %collective-permute-start = (bf16[1,8,16,256]{3,2,1,0:T(8,128)(2,1)S(1)}, bf16[1,8,16,256]{3,2,1,0:T(8,128)(2,1)S(1)}, u32[]{:S(2)}, u32[]{:S(2)}) collective-permute-start(bf16[1,8,16,256]{3,2,1,0:T(8,128)(2,1)S(1)} %bitcast.50), channel_id=1, source_target_pairs={{0,16},{16,0},{1,17},{17,1},{2,18},{18,2},{3,19},{19,3},{4,20},{20... | collective-permute-start | bytes 196616 | tf_op jit(solution)/shard_map/ppermute | solution.py:660
  11.2 4.0 %conv_middle.2.after_ref.middle_ref = bf16[1024,256]{1,0:T(8,128)(2,1)S(1)} custom-call(bf16[16,8,16,256]{3,2,1,0:T(8,128)(2,1)S(1)} %bitcast.25, bf16[27,256,256]{2,1,0:T(8,128)(2,1)S(1)} %get-tuple-element.39.w_ref), custom_call_target="tpu_custom_call" | custom-call | flops 3623878656 | bytes 1048576 | tf_op jit(solution)/shard_map/conv_middle/pallas_call | solution.py:35
  15.2 0.0 collective-permute-done
  15.3 0.6 zface.2
  15.8 3.5 %collective-permute-start.1 = (bf16[18,16,256]{2,1,0:T(8,128)(2,1)S(1)}, bf16[18,16,256]{2,1,0:T(8,128)(2,1)S(1)}, u32[]{:S(2)}, u32[]{:S(2)}) collective-permute-start(bf16[18,16,256]{2,1,0:T(8,128)(2,1)S(1)} %get-tuple-element.41), channel_id=1, source_target_pairs={{0,1},{1,2},{2,3},{4,5},{5,6},{6,7},{8,9},{9,10},{10,11},{12,13},{... | collective-permute-start | bytes 442376 | tf_op jit(solution)/shard_map/ppermute | solution.py:653
  19.3 1.3 collective-permute-start.2
  20.6 4.6 %conv_ends.2.after_ref.ends_ref = bf16[1024,256]{1,0:T(8,128)(2,1)S(1)} custom-call(s32[2]{0:T(128)S(1)} %add_convert_fusion.flags_ref, bf16[16,8,16,256]{3,2,1,0:T(8,128)(2,1)S(1)} %bitcast.28, bf16[8,16,256]{2,1,0:T(8,128)(2,1)S(1)} %bitcast.31, bf16[8,16,256]{2,1,0:T(8,128)(2,1)S(1)} %bitcast.32, bf16[27,256,256]{2,1,0:T(8,128)(2,1)S(1)} %get-tuple-element.39.w_ref), custom_call_target="tpu_custom_call" | custom-call | flops 3623878656 | bytes 1048576 | tf_op jit(solution)/shard_map/conv_ends/pallas_call | solution.py:35
  25.2 0.0 copy-start.4
  25.2 1.1 collective-permute-done.2.zhi_ref
  26.4 1.0 yface.2
  27.4 1.3 collective-permute-start.3
  28.7 1.3 collective-permute-start.4
  30.0 0.8 conv_z.2.zc_ref
  30.8 0.0 collective-permute-done.3.lo_ref
  30.8 2.9 %collective-permute-done.4.hi_ref = bf16[288,256]{1,0:T(8,128)(2,1)S(1)} collective-permute-done((bf16[288,256]{1,0:T(8,128)(2,1)S(1)}, bf16[288,256]{1,0:T(8,128)(2,1)S(1)}, u32[]{:S(2)}, u32[]{:S(2)}) %collective-permute-start.4) | collective-permute-done | bytes 147488 | tf_op jit(solution)/shard_map/ppermute | solution.py:654
  33.7 8.2 %conv_finish.2 = (f32[23040,256]{1,0:T(8,128)}, bf16[16,128,256]{2,1,0:T(8,128)(2,1)S(1)}) custom-call(s32[1]{0:T(128)} %bitcast.15.count_ref, s32[15]{0:T(128)S(1)} %bitcast.47, s32[15,1,128]{2,1,0:T(1,128)S(1)} %bitcast.42, bf16[1024,256]{1,0:T(8,128)(2,1)S(1)} %conv_middle.2.after_ref.middle_ref, bf16[1024,256]{1,0:T(8,128)(2,1)S(1)} %conv_ends.2.after_ref.ends_ref, ...), custom_call_target="tpu_custom_call" | custom-call | tf_op jit(solution)/shard_map/conv_finish/pallas_call | solution.py:35
  41.9 35.0 %all_to_all.30.recv_in_ref = bf16[16,128,256]{2,1,0:T(8,128)(2,1)} all-to-all(bf16[16,128,256]{2,1,0:T(8,128)(2,1)S(1)} %get-tuple-element.47), channel_id=1, replica_groups=mesh['gx'=2,'gy'=4,'gz'=4] {'gy','gz'}, dimensions={0} | all-to-all | bytes 2097152 | tf_op jit(solution)/shard_map/all_to_all | solution.py:801
  76.9 17.7 %owner_a.2 = (bf16[16,64,256]{2,1,0:T(8,128)(2,1)}, bf16[512,256]{1,0:T(8,128)(2,1)}, bf16[512,256]{1,0:T(8,128)(2,1)}, bf16[256,1024]{1,0:T(8,128)(2,1)}, bf16[1024,256]{1,0:T(8,128)(2,1)}, /*index=5*/s32[16]{0:T(128)}) custom-call(bf16[16,128,256]{2,1,0:T(8,128)(2,1)} %all_to_all.30.recv_in_ref, bf16[2,256,768]{2,1,0:T(8,128)(2,1)} %qkv_in_ref.3, ...), custom_call_target="tpu_custom_call" | custom-call | flops 8589934592 | bytes 1048576 | tf_op jit(solution)/shard_map/owner_a/pallas_call | solution.py:35
  94.6 3.8 %all-to-all-start.1 = ((bf16[16,64,256]{2,1,0:T(8,128)(2,1)}), bf16[16,64,256]{2,1,0:T(8,128)(2,1)S(1)}, u32[]{:S(2)}, u32[]{:S(2)}) async-start(bf16[16,64,256]{2,1,0:T(8,128)(2,1)} %get-tuple-element.48), calls=%async_computation.1 | async-start | bytes 1048576 | tf_op jit(solution)/shard_map/all_to_all | solution.py:803
  98.4 0.0 copy-start.2
  98.4 16.8 %owner_b.2 = bf16[16,64,256]{2,1,0:T(8,128)(2,1)} custom-call(s32[16]{0:T(128)} %get-tuple-element.49.pos_ref, bf16[512,256]{1,0:T(8,128)(2,1)} %get-tuple-element.50.x_in_ref, bf16[512,256]{1,0:T(8,128)(2,1)} %get-tuple-element.51.q_in_ref, bf16[256,1024]{1,0:T(8,128)(2,1)} %get-tuple-element.52.kt_in_ref, bf16[1024,256]{1,0:T(8,128)(2,1)} %get-tuple-element.53.v_in_ref, ...), custom_call_target="tpu_custom_call" | custom-call | flops 8589934592 | bytes 1048576 | tf_op jit(solution)/shard_map/owner_b/pallas_call | solution.py:35
  115.2 21.3 %all_to_all.31.back_b_ref = bf16[16,64,256]{2,1,0:T(8,128)(2,1)S(1)} all-to-all(bf16[16,64,256]{2,1,0:T(8,128)(2,1)} %owner_b.2), channel_id=1, replica_groups=mesh['gx'=2,'gy'=4,'gz'=4] {'gy','gz'}, dimensions={0} | all-to-all | bytes 1048576 | tf_op jit(solution)/shard_map/all_to_all | solution.py:803
  136.6 7.4 %place1.1 = (bf16[2048,256]{1,0:T(8,128)(2,1)S(1)}, bf16[1,128,256]{2,1,0:T(8,128)(2,1)S(1)}, bf16[2,288,256]{2,1,0:T(8,128)(2,1)S(1)}, bf16[27,256,256]{2,1,0:T(8,128)(2,1)S(1)}, f32[1920,256]{1,0:T(8,128)S(1)}) custom-call(s32[2]{0:T(128)S(1)} %add_convert_fusion.flags_ref, s32[1]{0:T(128)} %bitcast.16.count_ref, s32[15]{0:T(128)S(1)} %bitcast.48, ...), custom_call_target="tpu_custom_call" | custom-call | tf_op jit(solution)/shard_map/place1/pallas_call | solution.py:35
  143.9 0.7 collective-permute-start.5
  144.6 4.0 %conv_middle.3.after_ref.middle_ref = bf16[1024,256]{1,0:T(8,128)(2,1)S(1)} custom-call(bf16[16,8,16,256]{3,2,1,0:T(8,128)(2,1)S(1)} %bitcast.21, bf16[27,256,256]{2,1,0:T(8,128)(2,1)S(1)} %get-tuple-element.55.w_ref), custom_call_target="tpu_custom_call" | custom-call | flops 3623878656 | bytes 1048576 | tf_op jit(solution)/shard_map/conv_middle/pallas_call | solution.py:35
  148.7 0.6 zface.3
  149.3 1.8 collective-permute-start.6
  151.1 1.3 collective-permute-start.7
  152.4 4.6 %conv_ends.3.after_ref.ends_ref = bf16[1024,256]{1,0:T(8,128)(2,1)S(1)} custom-call(s32[2]{0:T(128)S(1)} %add_convert_fusion.flags_ref, bf16[16,8,16,256]{3,2,1,0:T(8,128)(2,1)S(1)} %bitcast.24, bf16[8,16,256]{2,1,0:T(8,128)(2,1)S(1)} %bitcast.37, bf16[8,16,256]{2,1,0:T(8,128)(2,1)S(1)} %bitcast.38, bf16[27,256,256]{2,1,0:T(8,128)(2,1)S(1)} %get-tuple-element.55.w_ref), custom_call_target="tpu_custom_call" | custom-call | flops 3623878656 | bytes 1048576 | tf_op jit(solution)/shard_map/conv_ends/pallas_call | solution.py:35
  157.0 0.0 copy-start.3
  157.0 1.4 collective-permute-done.7.zhi_ref
  158.4 1.0 yface.3
  159.4 1.3 collective-permute-start.8
  160.7 1.3 collective-permute-start.9
  162.0 0.8 conv_z.3.zc_ref
  162.8 2.6 collective-permute-done.9.hi_ref
  165.4 8.2 %conv_finish.3 = (f32[23040,256]{1,0:T(8,128)}, bf16[32,64,256]{2,1,0:T(8,128)(2,1)S(1)}) custom-call(s32[1]{0:T(128)} %bitcast.17.count_ref, s32[30]{0:T(128)S(1)} %bitcast.46, s32[15,1,128]{2,1,0:T(1,128)S(1)} %bitcast.44, bf16[1024,256]{1,0:T(8,128)(2,1)S(1)} %conv_middle.3.after_ref.middle_ref, bf16[1024,256]{1,0:T(8,128)(2,1)S(1)} %conv_ends.3.after_ref.ends_ref, ...), custom_call_target="tpu_custom_call" | custom-call | tf_op jit(solution)/shard_map/conv_finish/pallas_call | solution.py:35
  173.7 31.1 %all_to_all.32.recv_in_ref = bf16[32,64,256]{2,1,0:T(8,128)(2,1)} all-to-all(bf16[32,64,256]{2,1,0:T(8,128)(2,1)S(1)} %get-tuple-element.64), channel_id=1, replica_groups=mesh['gx'=2,'gy'=4,'gz'=4] {'gx','gz'}, dimensions={0} | all-to-all | bytes 2097152 | tf_op jit(solution)/shard_map/all_to_all | solution.py:801
  204.8 17.8 %owner_a.3 = (bf16[32,32,256]{2,1,0:T(8,128)(2,1)}, bf16[512,256]{1,0:T(8,128)(2,1)}, bf16[512,256]{1,0:T(8,128)(2,1)}, bf16[256,1024]{1,0:T(8,128)(2,1)}, bf16[1024,256]{1,0:T(8,128)(2,1)}, /*index=5*/s32[32]{0:T(128)}) custom-call(bf16[32,64,256]{2,1,0:T(8,128)(2,1)} %all_to_all.32.recv_in_ref, bf16[2,256,768]{2,1,0:T(8,128)(2,1)} %qkv_in_ref.3, ...), custom_call_target="tpu_custom_call" | custom-call | flops 8589934592 | bytes 1048576 | tf_op jit(solution)/shard_map/owner_a/pallas_call | solution.py:35
  222.6 3.5 %all-to-all-start.4 = ((bf16[32,32,256]{2,1,0:T(8,128)(2,1)}), bf16[32,32,256]{2,1,0:T(8,128)(2,1)S(1)}, u32[]{:S(2)}, u32[]{:S(2)}) async-start(bf16[32,32,256]{2,1,0:T(8,128)(2,1)} %get-tuple-element.65), calls=%async_computation.4 | async-start | bytes 1048576 | tf_op jit(solution)/shard_map/all_to_all | solution.py:803
  226.2 16.9 %owner_b.3 = bf16[32,32,256]{2,1,0:T(8,128)(2,1)} custom-call(s32[32]{0:T(128)} %get-tuple-element.66.pos_ref, bf16[512,256]{1,0:T(8,128)(2,1)} %get-tuple-element.67.x_in_ref, bf16[512,256]{1,0:T(8,128)(2,1)} %get-tuple-element.68.q_in_ref, bf16[256,1024]{1,0:T(8,128)(2,1)} %get-tuple-element.69.kt_in_ref, bf16[1024,256]{1,0:T(8,128)(2,1)} %get-tuple-element.70.v_in_ref, ...), custom_call_target="tpu_custom_call" | custom-call | flops 8589934592 | bytes 1048576 | tf_op jit(solution)/shard_map/owner_b/pallas_call | solution.py:35
  243.0 0.0 all-to-all-done.4.back_a_ref
  243.1 22.8 %all_to_all.33.back_b_ref = bf16[32,32,256]{2,1,0:T(8,128)(2,1)} all-to-all(bf16[32,32,256]{2,1,0:T(8,128)(2,1)} %owner_b.3), channel_id=1, replica_groups=mesh['gx'=2,'gy'=4,'gz'=4] {'gx','gz'}, dimensions={0} | all-to-all | bytes 1048576 | tf_op jit(solution)/shard_map/all_to_all | solution.py:803
  265.9 3.6 %restore.1 = f32[1920,256]{1,0:T(8,128)} custom-call(s32[1]{0:T(128)} %bitcast.18.count_ref, s32[30]{0:T(128)} %bitcast.45, f32[23040,256]{1,0:T(8,128)} %get-tuple-element.63.first_ref, bf16[32,32,256]{2,1,0:T(8,128)(2,1)} %copy-done.5, bf16[32,32,256]{2,1,0:T(8,128)(2,1)} %all_to_all.33.back_b_ref), custom_call_target="tpu_custom_call" | custom-call | tf_op jit(solution)/shard_map/restore/pallas_call | solution.py:35
  (12 shorter events, 0.0 us)
Async XLA Ops:
  0.7 1.5 copy-start
  2.3 0.7 copy-start.1
  8.1 7.1 %collective-permute-start = (bf16[1,8,16,256]{3,2,1,0:T(8,128)(2,1)S(1)}, bf16[1,8,16,256]{3,2,1,0:T(8,128)(2,1)S(1)}, u32[]{:S(2)}, u32[]{:S(2)}) collective-permute-start(bf16[1,8,16,256]{3,2,1,0:T(8,128)(2,1)S(1)} %bitcast.50), channel_id=1, source_target_pairs={{0,16},{16,0},{1,17},{17,1},{2,18},{18,2},{3,19},{19,3},{4,20},{20... | collective-permute-start | bytes 196616 | tf_op jit(solution)/shard_map/ppermute | solution.py:660
  15.8 9.4 %collective-permute-start.1 = (bf16[18,16,256]{2,1,0:T(8,128)(2,1)S(1)}, bf16[18,16,256]{2,1,0:T(8,128)(2,1)S(1)}, u32[]{:S(2)}, u32[]{:S(2)}) collective-permute-start(bf16[18,16,256]{2,1,0:T(8,128)(2,1)S(1)} %get-tuple-element.41), channel_id=1, source_target_pairs={{0,1},{1,2},{2,3},{4,5},{5,6},{6,7},{8,9},{9,10},{10,11},{12,13},{... | collective-permute-start | bytes 442376 | tf_op jit(solution)/shard_map/ppermute | solution.py:653
  19.3 7.0 %collective-permute-start.2 = (bf16[18,16,256]{2,1,0:T(8,128)(2,1)S(1)}, bf16[18,16,256]{2,1,0:T(8,128)(2,1)S(1)}, u32[]{:S(2)}, u32[]{:S(2)}) collective-permute-start(bf16[18,16,256]{2,1,0:T(8,128)(2,1)S(1)} %get-tuple-element.42), channel_id=1, source_target_pairs={{1,0},{2,1},{3,2},{5,4},{6,5},{7,6},{9,8},{10,9},{11,10},{13,12},{... | collective-permute-start | bytes 442376 | tf_op jit(solution)/shard_map/ppermute | solution.py:654
  25.2 8.5 %copy-start.4 = (s32[1,1,1,15]{3,2,1,0:T(1,128)S(1)}, s32[1,1,1,15]{3,2,1,0:T(1,128)}, u32[]{:S(2)}) copy-start(s32[1,1,1,15]{3,2,1,0:T(1,128)} %param.13) | copy-start | bytes 184
  27.4 3.4 %collective-permute-start.3 = (bf16[288,256]{1,0:T(8,128)(2,1)S(1)}, bf16[288,256]{1,0:T(8,128)(2,1)S(1)}, u32[]{:S(2)}, u32[]{:S(2)}) collective-permute-start(bf16[288,256]{1,0:T(8,128)(2,1)S(1)} %get-tuple-element.44), channel_id=1, source_target_pairs={{0,4},{4,8},{8,12},{1,5},{5,9},{9,13},{2,6},{6,10},{10,14},{3,7},{... | collective-permute-start | bytes 442376 | tf_op jit(solution)/shard_map/ppermute | solution.py:653
  28.7 5.0 %collective-permute-start.4 = (bf16[288,256]{1,0:T(8,128)(2,1)S(1)}, bf16[288,256]{1,0:T(8,128)(2,1)S(1)}, u32[]{:S(2)}, u32[]{:S(2)}) collective-permute-start(bf16[288,256]{1,0:T(8,128)(2,1)S(1)} %get-tuple-element.45), channel_id=1, source_target_pairs={{4,0},{8,4},{12,8},{5,1},{9,5},{13,9},{6,2},{10,6},{14,10},{7,3},{... | collective-permute-start | bytes 442376 | tf_op jit(solution)/shard_map/ppermute | solution.py:654
  94.6 20.6 %all-to-all-start.1 = ((bf16[16,64,256]{2,1,0:T(8,128)(2,1)}), bf16[16,64,256]{2,1,0:T(8,128)(2,1)S(1)}, u32[]{:S(2)}, u32[]{:S(2)}) async-start(bf16[16,64,256]{2,1,0:T(8,128)(2,1)} %get-tuple-element.48), calls=%async_computation.1 | async-start | bytes 1048576 | tf_op jit(solution)/shard_map/all_to_all | solution.py:803
  98.4 38.2 %copy-start.2 = (s32[1,1,1,1920]{3,2,1,0:T(1,128)S(1)}, s32[1,1,1,1920]{3,2,1,0:T(1,128)}, u32[]{:S(2)}) copy-start(s32[1,1,1,1920]{3,2,1,0:T(1,128)} %param.11) | copy-start | bytes 23044
  143.9 4.8 %collective-permute-start.5 = (bf16[1,8,16,256]{3,2,1,0:T(8,128)(2,1)S(1)}, bf16[1,8,16,256]{3,2,1,0:T(8,128)(2,1)S(1)}, u32[]{:S(2)}, u32[]{:S(2)}) collective-permute-start(bf16[1,8,16,256]{3,2,1,0:T(8,128)(2,1)S(1)} %bitcast.49), channel_id=1, source_target_pairs={{0,16},{16,0},{1,17},{17,1},{2,18},{18,2},{3,19},{19,3},{4,20},{20... | collective-permute-start | bytes 196616 | tf_op jit(solution)/shard_map/ppermute | solution.py:660
  149.3 7.7 %collective-permute-start.6 = (bf16[18,16,256]{2,1,0:T(8,128)(2,1)S(1)}, bf16[18,16,256]{2,1,0:T(8,128)(2,1)S(1)}, u32[]{:S(2)}, u32[]{:S(2)}) collective-permute-start(bf16[18,16,256]{2,1,0:T(8,128)(2,1)S(1)} %get-tuple-element.57), channel_id=1, source_target_pairs={{0,1},{1,2},{2,3},{4,5},{5,6},{6,7},{8,9},{9,10},{10,11},{12,13},{... | collective-permute-start | bytes 442376 | tf_op jit(solution)/shard_map/ppermute | solution.py:653
  151.1 7.3 %collective-permute-start.7 = (bf16[18,16,256]{2,1,0:T(8,128)(2,1)S(1)}, bf16[18,16,256]{2,1,0:T(8,128)(2,1)S(1)}, u32[]{:S(2)}, u32[]{:S(2)}) collective-permute-start(bf16[18,16,256]{2,1,0:T(8,128)(2,1)S(1)} %get-tuple-element.58), channel_id=1, source_target_pairs={{1,0},{2,1},{3,2},{5,4},{6,5},{7,6},{9,8},{10,9},{11,10},{13,12},{... | collective-permute-start | bytes 442376 | tf_op jit(solution)/shard_map/ppermute | solution.py:654
  157.0 8.4 %copy-start.3 = (s32[1,1,1,30]{3,2,1,0:T(1,128)S(1)}, s32[1,1,1,30]{3,2,1,0:T(1,128)}, u32[]{:S(2)}) copy-start(s32[1,1,1,30]{3,2,1,0:T(1,128)} %param.14) | copy-start | bytes 364
  159.4 3.4 %collective-permute-start.8 = (bf16[288,256]{1,0:T(8,128)(2,1)S(1)}, bf16[288,256]{1,0:T(8,128)(2,1)S(1)}, u32[]{:S(2)}, u32[]{:S(2)}) collective-permute-start(bf16[288,256]{1,0:T(8,128)(2,1)S(1)} %get-tuple-element.60), channel_id=1, source_target_pairs={{0,4},{4,8},{8,12},{1,5},{5,9},{9,13},{2,6},{6,10},{10,14},{3,7},{... | collective-permute-start | bytes 442376 | tf_op jit(solution)/shard_map/ppermute | solution.py:653
  160.7 4.7 %collective-permute-start.9 = (bf16[288,256]{1,0:T(8,128)(2,1)S(1)}, bf16[288,256]{1,0:T(8,128)(2,1)S(1)}, u32[]{:S(2)}, u32[]{:S(2)}) collective-permute-start(bf16[288,256]{1,0:T(8,128)(2,1)S(1)} %get-tuple-element.61), channel_id=1, source_target_pairs={{4,0},{8,4},{12,8},{5,1},{9,5},{13,9},{6,2},{10,6},{14,10},{7,3},{... | collective-permute-start | bytes 442376 | tf_op jit(solution)/shard_map/ppermute | solution.py:654
  222.6 20.4 %all-to-all-start.4 = ((bf16[32,32,256]{2,1,0:T(8,128)(2,1)}), bf16[32,32,256]{2,1,0:T(8,128)(2,1)S(1)}, u32[]{:S(2)}, u32[]{:S(2)}) async-start(bf16[32,32,256]{2,1,0:T(8,128)(2,1)} %get-tuple-element.65), calls=%async_computation.4 | async-start | bytes 1048576 | tf_op jit(solution)/shard_map/all_to_all | solution.py:803
  243.1 22.8 %copy-start.5 = (bf16[32,32,256]{2,1,0:T(8,128)(2,1)}, bf16[32,32,256]{2,1,0:T(8,128)(2,1)S(1)}, u32[]{:S(2)}) copy-start(bf16[32,32,256]{2,1,0:T(8,128)(2,1)S(1)} %all-to-all-done.4.back_a_ref) | copy-start | bytes 1572868

commit v2 on v1

--- a/solution.py
+++ b/solution.py
@@ -19,7 +19,7 @@
 PLANE = PX * PZ
 EPS = 1e-05
 CLIP = 3e38
-HELD = 12
+HELD = 24
 F32 = jnp.float32
 BF16 = jnp.bfloat16
 SMEM = pltpu.MemorySpace.SMEM
@@ -80,10 +80,9 @@
 
 
 def cell_of(voxel):
-    x = voxel // (VY * VZ)
-    y = (voxel // VZ) % VY
-    z = voxel % VZ
-    return (x * VZ + z) * VY + y
+    y = (voxel >> bits(VZ)) & (VY - 1)
+    z = voxel & (VZ - 1)
+    return ((voxel >> bits(VY * VZ)) << bits(VY * VZ)) | (z << bits(VY)) | y
 
 
 def voxel_row(vox_ref):
@@ -164,7 +163,7 @@
     part = unit // len(backs)
     for k, back_ref in enumerate(backs):
         rows = pl.ds(pl.multiple_of(u * unit + k * part, part), part)
-        total = first_ref[rows, :] + back_ref[slot].astype(F32)
+        total = first_ref[rows, :].astype(F32) + back_ref[slot].astype(F32)
         yield rows, jnp.where(alive, total, 0.0)
 
 
@@ -339,15 +338,54 @@
         out_ref[face] = shift_sum(accs)
 
 
+def block_cells(vox_ref, j):
+    block = vox_ref.shape[-1]
+    cells = cell_of(vox_ref[j]).astype(F32)
+    return jnp.transpose(jnp.broadcast_to(cells, (block, block))).astype(jnp.int32)
+
+
+def bits(count):
+    assert count & (count - 1) == 0
+    return count.bit_length() - 1
+
+
+def hot_row_groups(vox_ref):
+    return next(g for g in (3, 2, 1) if vox_ref.shape[0] % g == 0)
+
+
+def gather_kernel(planes, vox_ref, middle_ref, ends_ref, zc_ref, out_ref, table_ref):
+    per_x = VZ * VY
+    edge = planes * per_x
+    table_ref[0:edge] = ends_ref[0:edge]
+    table_ref[edge : CELLS - edge] = middle_ref[...]
+    table_ref[CELLS - edge : CELLS] = ends_ref[edge:]
+    for face, z in ((0, 0), (1, VZ - 1)):
+        for x in range(VX):
+            rows = slice(x * per_x + z * VY, x * per_x + (z + 1) * VY)
+            table_ref[rows] = (table_ref[rows].astype(F32) + zc_ref[face, x]).astype(BF16)
+    blocks, _, block = vox_ref.shape
+    group = hot_row_groups(vox_ref)
+
+    def hot_rows(j):
+        cell = block_cells(vox_ref, j)
+        lane = iota((block, block), 1)
+        return jnp.concatenate([onehot(cell == lane + k * block) for k in range(CELLS // block)], axis=1)
+
+    def one(g, c):
+        hot = jnp.concatenate([hot_rows(g * group + i) for i in range(group)], axis=0)
+        rows = pl.ds(pl.multiple_of(g * group * block, group * block), group * block)
+        out_ref[rows, :] = jnp.dot(hot, table_ref[...], preferred_element_type=F32)
+        return c
+
+    lax.fori_loop(0, blocks // group, one, 0)
+
+
 def conv_finish_kernel(
-    planes,
     route,
     count_ref,
     dest_ref,
     vox_ref,
-    middle_ref,
-    ends_ref,
-    zc_ref,
+    main_ref,
     lo_ref,
     hi_ref,
     w_ref,
@@ -361,19 +399,10 @@
     fsems,
 ):
     owners, capacity, per_owner, units_per_block, unit = route
-    channels = middle_ref.shape[-1]
+    channels = main_ref.shape[-1]
     assign_slots(dest_ref, count_ref, slot_ref, used_ref, owners, capacity, per_owner, units_per_block)
     for s in range(owners * capacity):
         send_ref[s, 0:16] = jnp.full((16, channels), jnp.inf, BF16)
-    per_x = VZ * VY
-    edge = planes * per_x
-    table_ref[0:edge] = ends_ref[0:edge]
-    table_ref[edge : CELLS - edge] = middle_ref[...]
-    table_ref[CELLS - edge : CELLS] = ends_ref[edge:]
-    for face, z in ((0, 0), (1, VZ - 1)):
-        for x in range(VX):
-            rows = slice(x * per_x + z * VY, x * per_x + (z + 1) * VY)
-            table_ref[rows] = (table_ref[rows].astype(F32) + zc_ref[face, x]).astype(BF16)
     plane_rows = VX * PZ
     for face, plane_ref in ((0, lo_ref), (1, hi_ref)):
         plane = plane_ref[...].reshape(PX, PZ, channels)
@@ -382,33 +411,29 @@
         parts = [shifted[dc][da : da + VX].reshape(plane_rows, channels) for da in range(3) for dc in range(3)]
         rhs = jnp.concatenate([tap(w_ref, da, 2 * face, dc) for da in range(3) for dc in range(3)], axis=0)
         out = jnp.dot(jnp.concatenate(parts, axis=1), rhs, preferred_element_type=F32)
-        table_ref[CELLS + face * plane_rows : CELLS + (face + 1) * plane_rows] = out.astype(BF16)
+        table_ref[face * plane_rows : (face + 1) * plane_rows] = out.astype(BF16)
     blocks, _, block = vox_ref.shape
-    group = next(g for g in (3, 2, 1) if blocks % g == 0)
+    group = hot_row_groups(vox_ref)
     live = count_ref[0]
 
     def hot_rows(j):
-        v = vox_ref[j]
-        vt = jnp.transpose(jnp.broadcast_to(v.astype(F32), (block, block))).astype(jnp.int32)
-        x = vt // (VY * VZ)
-        y = (vt // VZ) % VY
-        z = vt % VZ
-        main = (x * VZ + z) * VY + y
-        lo = jnp.where(y == 0, CELLS + x * PZ + z, -1)
-        hi = jnp.where(y == VY - 1, CELLS + plane_rows + x * PZ + z, -1)
+        cell = block_cells(vox_ref, j)
+        y = cell & (VY - 1)
+        spot = (cell >> bits(VY)) + (cell >> bits(VY * VZ)) * (PZ - VZ)
+        lo = jnp.where(y == 0, spot, -1)
+        hi = jnp.where(y == VY - 1, spot + plane_rows, -1)
         lane = iota((block, block), 1)
         pieces = []
-        for k in range((CELLS + 2 * plane_rows) // block):
-            ids = main if k * block < CELLS else (lo if k * block < CELLS + plane_rows else hi)
-            pieces.append(onehot(ids == lane + k * block))
+        for k in range(2 * plane_rows // block):
+            pieces.append(onehot((lo if k * block < plane_rows else hi) == lane + k * block))
         return jnp.concatenate(pieces, axis=1)
 
     def one(g, c):
         hot = jnp.concatenate([hot_rows(g * group + i) for i in range(group)], axis=0)
-        gathered = jnp.dot(hot, table_ref[...], preferred_element_type=F32)
         rows = pl.ds(pl.multiple_of(g * group * block, group * block), group * block)
+        gathered = main_ref[rows, :] + jnp.dot(hot, table_ref[...], preferred_element_type=F32)
         first = stream_ref[rows, :] + layer_norm(gathered)
-        first_vmem[rows, :] = first
+        first_vmem[rows, :] = first.astype(BF16)
         pltpu.make_async_copy(first_vmem.at[rows], first_ref.at[rows], fsems.at[g]).start()
         packed = jnp.clip(first, -CLIP, CLIP).astype(BF16)
         for i in range(group):
@@ -428,7 +453,7 @@
         pltpu.make_async_copy(first_vmem.at[rows], first_ref.at[rows], fsems.at[g]).wait()
 
 
-def attend_and_feed(x_ref, q_ref, kt_ref, va_ref, vb_ref, proj_ref, up_ref, down_ref, heads_ref, s0_ref, s1_ref, delta_ref):
+def attend_and_feed(x_ref, q_ref, kt_ref, va_ref, vb_ref, proj_ref, up_ref, down_ref, heads_ref, s0_ref, s1_ref, delta_ref, awaited):
     tile, channels = q_ref.shape
     half = channels // 2
     width = channels // HEADS
@@ -458,6 +483,8 @@
         return c
 
     lax.fori_loop(0, half // width, head, 0)
+    for copy in awaited:
+        copy.wait()
     x = x_ref[0:tile, :].astype(F32)
     update = jnp.dot(heads_ref[...].astype(BF16), proj_ref[...], preferred_element_type=F32)
     normed = layer_norm(x + update).astype(BF16)
@@ -554,10 +581,8 @@
     for copy in handed:
         copy.start()
     with_ones(v_ref, va_ref, vb_ref)
-    for copy in weights[1:]:
-        copy.wait()
     attend_and_feed(
-        xa_ref, qa_ref, kt_ref, va_ref, vb_ref, proj_ref, up_ref, down_ref, heads_ref, s0_ref, s1_ref, delta_ref
+        xa_ref, qa_ref, kt_ref, va_ref, vb_ref, proj_ref, up_ref, down_ref, heads_ref, s0_ref, s1_ref, delta_ref, weights[1:]
     )
     for copy in handed + answer_copies(pos_ref, delta_ref, out_ref, osems):
         copy.wait()
@@ -597,10 +622,13 @@
     copies = [pltpu.make_async_copy(src, dst, sems.at[k]) for k, (src, dst) in enumerate(pairs)]
     for copy in copies + weights:
         copy.start()
-    for copy in copies + weights:
+    for copy in copies[:3]:
         copy.wait()
     with_ones(v_ref, va_ref, vb_ref)
-    attend_and_feed(x_ref, q_ref, kt_ref, va_ref, vb_ref, proj_ref, up_ref, down_ref, heads_ref, s0_ref, s1_ref, delta_ref)
+    awaited = copies[3:] + weights
+    attend_and_feed(
+        x_ref, q_ref, kt_ref, va_ref, vb_ref, proj_ref, up_ref, down_ref, heads_ref, s0_ref, s1_ref, delta_ref, awaited
+    )
     for copy in answer_copies(pos_ref, delta_ref, out_ref, osems):
         copy.wait()
 
@@ -730,7 +758,7 @@
                 [(flags, "s"), (count, "s"), (dests[layer - 1], "s"), (vox_block, "v"), (first, "h")]
                 + [(b, "v") for b in backs]
                 + [(conv_weight, "h")],
-                [rows_scratch, stream_scratch] + route_scratch(layer - 1) + [row_sems, weight_sems],
+                [rows_scratch, rows_scratch] + route_scratch(layer - 1) + [row_sems, weight_sems],
                 "place1",
                 44,
             )
@@ -782,16 +810,25 @@
             24,
             half_conv // 4,
         )
+        gathered = call(
+            functools.partial(gather_kernel, planes),
+            [(sds((slot_count, channels), F32), "v")],
+            [(vox_block, "v"), (middle, "v"), (ends, "v"), (zc, "v")],
+            [pltpu.VMEM((CELLS, channels), BF16)],
+            "gather",
+            24,
+            half_conv // 2,
+        )
         slots = owners * capacity
         groups = blocks // next(g for g in (3, 2, 1) if blocks % g == 0)
         first, send = call(
-            functools.partial(conv_finish_kernel, planes, route),
-            [(sds((HELD * slot_count, channels), F32), "h"), (sds((slots, unit, channels), BF16), "v")],
-            [(count, "s"), (dests[layer], "s"), (vox_block, "v"), (middle, "v"), (ends, "v"), (zc, "v")]
+            functools.partial(conv_finish_kernel, route),
+            [(sds((HELD * slot_count, channels), BF16), "h"), (sds((slots, unit, channels), BF16), "v")],
+            [(count, "s"), (dests[layer], "s"), (vox_block, "v"), (gathered, "v")]
             + [(ylo, "v"), (yhi, "v"), (weights, "v"), (stream, "v")],
             [
-                pltpu.VMEM((CELLS + 2 * VX * PZ, channels), BF16),
-                stream_scratch,
+                pltpu.VMEM((2 * VX * PZ, channels), BF16),
+                rows_scratch,
             ]
             + route_scratch(layer)
             + [pltpu.SemaphoreType.DMA((groups,))],
@@ -805,7 +842,7 @@
         functools.partial(restore_kernel, routes[1]),
         [(sds((slot_count, channels), F32), "h")],
         [(count, "s"), (dests[1], "s"), (first, "h")] + [(b, "v") for b in backs],
-        [stream_scratch, stream_scratch] + route_scratch(1) + [row_sems, row_sems],
+        [rows_scratch, stream_scratch] + route_scratch(1) + [row_sems, row_sems],
         "restore",
         60,
     )

time: 271 us -> 264 us (0.974)
  waiting for transfers between devices: 7.99 us -> 2.57 us
    ppermute x4, waiting for transfers between devices: 7.96 us -> 2.55 us  [up_down(): lax.ppermute(low_face, axis, [((i + 1) % count, i) for i in range(ends)])]
    pallas_call x19 -> x21, Pallas kernels: 124 us -> 122 us  [call(): pl.pallas_call(kernel, out_shape=tuple((shape for shape, _ in outs)), gri...]
  transfers between devices with their start and end apart: 12 -> 12, of which waited for: 4 -> 2; matrix products, arithmetic and copies ran while one was open for 0% -> 0% of each run, Pallas kernels for 19% -> 22%
where the time goes in v2:
time: 264 us; the launch traced here: 263 us
  Pallas kernels  122 us (46%)
  blocking collectives  111 us (42%)
  starting transfers between devices  23.9 us (9%)
    pallas_call x21, Pallas kernels, call(): pl.pallas_call(kernel, out_shape=tuple((shape for shape, _ in outs)), gri...  122 us
    all_to_all x2, blocking collectives, body(): lax.all_to_all(send, axes[layer], split_axis=0, concat_axis=0, tiled=True)  66.5 us
    all_to_all x2, blocking collectives, body(): lax.all_to_all(a, axes[layer], split_axis=0, concat_axis=0, tiled=True)  44.2 us
    ppermute x4, starting transfers between devices, up_down(): lax.ppermute(high_face, axis, [(i, (i + 1) % count) for i in range(ends)])  7.88 us
    all_to_all x2, starting transfers between devices, body(): lax.all_to_all(a, axes[layer], split_axis=0, concat_axis=0, tiled=True)  7.27 us
  transfers between devices with their start and end apart: 12, of which 2 were waited for; matrix products, arithmetic and copies ran while one was open for 0% of the time, Pallas kernels for 22%

profile of v2, /device:TPU:0, one launch (start us, length us, event | category | flops | bytes accessed | tf_op | source)
XLA Modules:
  0.0 263.1 jit_solution(3197966170044376800)
XLA Ops:
  0.7 0.1 add_convert_fusion.flags_ref
  0.7 1.5 copy-done
  2.3 0.7 copy-done.1
  3.0 5.1 %place0.1 = (bf16[2048,256]{1,0:T(8,128)(2,1)S(1)}, bf16[1,128,256]{2,1,0:T(8,128)(2,1)S(1)}, bf16[2,288,256]{2,1,0:T(8,128)(2,1)S(1)}, bf16[27,256,256]{2,1,0:T(8,128)(2,1)S(1)}) custom-call(s32[2]{0:T(128)S(1)} %add_convert_fusion.flags_ref, s32[1]{0:T(128)} %bitcast.14.count_ref, s32[15,1,128]{2,1,0:T(1,128)S(1)} %bitcast.41, f32[1920,256]{1,0:T(8,128)S(1)} %bitcast.19, ...), custom_call_target="tpu_custom_call" | custom-call | tf_op jit(solution)/shard_map/place0/pallas_call | solution.py:35
  8.0 3.1 %collective-permute-start = (bf16[1,8,16,256]{3,2,1,0:T(8,128)(2,1)S(1)}, bf16[1,8,16,256]{3,2,1,0:T(8,128)(2,1)S(1)}, u32[]{:S(2)}, u32[]{:S(2)}) collective-permute-start(bf16[1,8,16,256]{3,2,1,0:T(8,128)(2,1)S(1)} %bitcast.52), channel_id=1, source_target_pairs={{0,16},{16,0},{1,17},{17,1},{2,18},{18,2},{3,19},{19,3},{4,20},{20... | collective-permute-start | bytes 196616 | tf_op jit(solution)/shard_map/ppermute | solution.py:688
  11.1 4.0 %conv_middle.2.after_ref.middle_ref = bf16[1024,256]{1,0:T(8,128)(2,1)S(1)} custom-call(bf16[16,8,16,256]{3,2,1,0:T(8,128)(2,1)S(1)} %bitcast.25, bf16[27,256,256]{2,1,0:T(8,128)(2,1)S(1)} %get-tuple-element.39.w_ref), custom_call_target="tpu_custom_call" | custom-call | flops 3623878656 | bytes 1048576 | tf_op jit(solution)/shard_map/conv_middle/pallas_call | solution.py:35
  15.1 0.0 collective-permute-done
  15.2 0.6 zface.2
  15.7 3.5 %collective-permute-start.1 = (bf16[18,16,256]{2,1,0:T(8,128)(2,1)S(1)}, bf16[18,16,256]{2,1,0:T(8,128)(2,1)S(1)}, u32[]{:S(2)}, u32[]{:S(2)}) collective-permute-start(bf16[18,16,256]{2,1,0:T(8,128)(2,1)S(1)} %get-tuple-element.41), channel_id=1, source_target_pairs={{0,1},{1,2},{2,3},{4,5},{5,6},{6,7},{8,9},{9,10},{10,11},{12,13},{... | collective-permute-start | bytes 442376 | tf_op jit(solution)/shard_map/ppermute | solution.py:681
  19.2 1.3 collective-permute-start.2
  20.5 4.6 %conv_ends.2.ends_ref.after_ref = bf16[1024,256]{1,0:T(8,128)(2,1)S(1)} custom-call(s32[2]{0:T(128)S(1)} %add_convert_fusion.flags_ref, bf16[16,8,16,256]{3,2,1,0:T(8,128)(2,1)S(1)} %bitcast.28, bf16[8,16,256]{2,1,0:T(8,128)(2,1)S(1)} %bitcast.31, bf16[8,16,256]{2,1,0:T(8,128)(2,1)S(1)} %bitcast.32, bf16[27,256,256]{2,1,0:T(8,128)(2,1)S(1)} %get-tuple-element.39.w_ref), custom_call_target="tpu_custom_call" | custom-call | flops 3623878656 | bytes 1048576 | tf_op jit(solution)/shard_map/conv_ends/pallas_call | solution.py:35
  25.1 1.1 collective-permute-done.2.zhi_ref
  26.3 1.0 yface.2
  27.3 1.3 collective-permute-start.3
  28.6 1.3 collective-permute-start.4
  29.9 0.8 conv_z.2.zc_ref
  30.7 0.0 copy-start.4
  30.7 3.3 %gather.2.main_ref = f32[1920,256]{1,0:T(8,128)S(1)} custom-call(s32[15,1,128]{2,1,0:T(1,128)S(1)} %bitcast.42, bf16[1024,256]{1,0:T(8,128)(2,1)S(1)} %conv_middle.2.after_ref.middle_ref, bf16[1024,256]{1,0:T(8,128)(2,1)S(1)} %conv_ends.2.ends_ref.after_ref, f32[2,16,16,256]{3,2,1,0:T(8,128)S(1)} %conv_z.2.zc_ref), custom_call_target="tpu_custom_call" | custom-call | flops 1811939328 | bytes 1048576 | tf_op jit(solution)/shard_map/gather/pallas_call | solution.py:35
  34.0 0.0 collective-permute-done.3.lo_ref
  34.0 5.0 %conv_finish.2 = (bf16[46080,256]{1,0:T(8,128)(2,1)}, bf16[16,128,256]{2,1,0:T(8,128)(2,1)S(1)}) custom-call(s32[1]{0:T(128)} %bitcast.15.count_ref, s32[15]{0:T(128)S(1)} %bitcast.49, s32[15,1,128]{2,1,0:T(1,128)S(1)} %bitcast.43, f32[1920,256]{1,0:T(8,128)S(1)} %gather.2.main_ref, bf16[288,256]{1,0:T(8,128)(2,1)S(1)} %collective-permute-done.3.lo_ref, ...), custom_call_target="tpu_custom_call" | custom-call | tf_op jit(solution)/shard_map/conv_finish/pallas_call | solution.py:35
  39.0 35.6 %all_to_all.30.recv_in_ref = bf16[16,128,256]{2,1,0:T(8,128)(2,1)} all-to-all(bf16[16,128,256]{2,1,0:T(8,128)(2,1)S(1)} %get-tuple-element.47), channel_id=1, replica_groups=mesh['gx'=2,'gy'=4,'gz'=4] {'gy','gz'}, dimensions={0} | all-to-all | bytes 2097152 | tf_op jit(solution)/shard_map/all_to_all | solution.py:838
  74.6 17.5 %owner_a.2 = (bf16[16,64,256]{2,1,0:T(8,128)(2,1)}, bf16[512,256]{1,0:T(8,128)(2,1)}, bf16[512,256]{1,0:T(8,128)(2,1)}, bf16[256,1024]{1,0:T(8,128)(2,1)}, bf16[1024,256]{1,0:T(8,128)(2,1)}, /*index=5*/s32[16]{0:T(128)}) custom-call(bf16[16,128,256]{2,1,0:T(8,128)(2,1)} %all_to_all.30.recv_in_ref, bf16[2,256,768]{2,1,0:T(8,128)(2,1)} %qkv_in_ref.3, ...), custom_call_target="tpu_custom_call" | custom-call | flops 8589934592 | bytes 1048576 | tf_op jit(solution)/shard_map/owner_a/pallas_call | solution.py:35
  92.1 3.8 %all-to-all-start.1 = ((bf16[16,64,256]{2,1,0:T(8,128)(2,1)}), bf16[16,64,256]{2,1,0:T(8,128)(2,1)S(1)}, u32[]{:S(2)}, u32[]{:S(2)}) async-start(bf16[16,64,256]{2,1,0:T(8,128)(2,1)} %get-tuple-element.48), calls=%async_computation.1 | async-start | bytes 1048576 | tf_op jit(solution)/shard_map/all_to_all | solution.py:840
  95.9 0.0 copy-start.2
  95.9 16.5 %owner_b.2 = bf16[16,64,256]{2,1,0:T(8,128)(2,1)} custom-call(s32[16]{0:T(128)} %get-tuple-element.49.pos_ref, bf16[512,256]{1,0:T(8,128)(2,1)} %get-tuple-element.50.x_in_ref, bf16[512,256]{1,0:T(8,128)(2,1)} %get-tuple-element.51.q_in_ref, bf16[256,1024]{1,0:T(8,128)(2,1)} %get-tuple-element.52.kt_in_ref, bf16[1024,256]{1,0:T(8,128)(2,1)} %get-tuple-element.53.v_in_ref, ...), custom_call_target="tpu_custom_call" | custom-call | flops 8589934592 | bytes 1048576 | tf_op jit(solution)/shard_map/owner_b/pallas_call | solution.py:35
  112.4 21.3 %all_to_all.31.back_b_ref = bf16[16,64,256]{2,1,0:T(8,128)(2,1)S(1)} all-to-all(bf16[16,64,256]{2,1,0:T(8,128)(2,1)} %owner_b.2), channel_id=1, replica_groups=mesh['gx'=2,'gy'=4,'gz'=4] {'gy','gz'}, dimensions={0} | all-to-all | bytes 1048576 | tf_op jit(solution)/shard_map/all_to_all | solution.py:840
  133.8 7.1 %place1.1 = (bf16[2048,256]{1,0:T(8,128)(2,1)S(1)}, bf16[1,128,256]{2,1,0:T(8,128)(2,1)S(1)}, bf16[2,288,256]{2,1,0:T(8,128)(2,1)S(1)}, bf16[27,256,256]{2,1,0:T(8,128)(2,1)S(1)}, f32[1920,256]{1,0:T(8,128)S(1)}) custom-call(s32[2]{0:T(128)S(1)} %add_convert_fusion.flags_ref, s32[1]{0:T(128)} %bitcast.16.count_ref, s32[15]{0:T(128)S(1)} %bitcast.50, ...), custom_call_target="tpu_custom_call" | custom-call | tf_op jit(solution)/shard_map/place1/pallas_call | solution.py:35
  140.9 0.5 collective-permute-start.5
  141.4 4.0 %conv_middle.3.after_ref.middle_ref = bf16[1024,256]{1,0:T(8,128)(2,1)S(1)} custom-call(bf16[16,8,16,256]{3,2,1,0:T(8,128)(2,1)S(1)} %bitcast.21, bf16[27,256,256]{2,1,0:T(8,128)(2,1)S(1)} %get-tuple-element.55.w_ref), custom_call_target="tpu_custom_call" | custom-call | flops 3623878656 | bytes 1048576 | tf_op jit(solution)/shard_map/conv_middle/pallas_call | solution.py:35
  145.4 0.0 collective-permute-done.5
  145.4 0.6 zface.3
  146.0 1.8 collective-permute-start.6
  147.8 1.3 collective-permute-start.7
  149.1 4.6 %conv_ends.3.ends_ref.after_ref = bf16[1024,256]{1,0:T(8,128)(2,1)S(1)} custom-call(s32[2]{0:T(128)S(1)} %add_convert_fusion.flags_ref, bf16[16,8,16,256]{3,2,1,0:T(8,128)(2,1)S(1)} %bitcast.24, bf16[8,16,256]{2,1,0:T(8,128)(2,1)S(1)} %bitcast.37, bf16[8,16,256]{2,1,0:T(8,128)(2,1)S(1)} %bitcast.38, bf16[27,256,256]{2,1,0:T(8,128)(2,1)S(1)} %get-tuple-element.55.w_ref), custom_call_target="tpu_custom_call" | custom-call | flops 3623878656 | bytes 1048576 | tf_op jit(solution)/shard_map/conv_ends/pallas_call | solution.py:35
  153.7 1.4 collective-permute-done.7.zhi_ref
  155.1 1.0 yface.3
  156.2 1.3 collective-permute-start.8
  157.5 1.3 collective-permute-start.9
  158.8 0.8 conv_z.3.zc_ref
  159.6 0.0 copy-start.3
  159.6 3.2 %gather.3.main_ref = f32[1920,256]{1,0:T(8,128)S(1)} custom-call(s32[15,1,128]{2,1,0:T(1,128)S(1)} %bitcast.45, bf16[1024,256]{1,0:T(8,128)(2,1)S(1)} %conv_middle.3.after_ref.middle_ref, bf16[1024,256]{1,0:T(8,128)(2,1)S(1)} %conv_ends.3.ends_ref.after_ref, f32[2,16,16,256]{3,2,1,0:T(8,128)S(1)} %conv_z.3.zc_ref), custom_call_target="tpu_custom_call" | custom-call | flops 1811939328 | bytes 1048576 | tf_op jit(solution)/shard_map/gather/pallas_call | solution.py:35
  162.9 5.0 %conv_finish.3 = (bf16[46080,256]{1,0:T(8,128)(2,1)}, bf16[32,64,256]{2,1,0:T(8,128)(2,1)S(1)}) custom-call(s32[1]{0:T(128)} %bitcast.17.count_ref, s32[30]{0:T(128)S(1)} %bitcast.48, s32[15,1,128]{2,1,0:T(1,128)S(1)} %bitcast.46, f32[1920,256]{1,0:T(8,128)S(1)} %gather.3.main_ref, bf16[288,256]{1,0:T(8,128)(2,1)S(1)} %collective-permute-done.8.lo_ref, ...), custom_call_target="tpu_custom_call" | custom-call | tf_op jit(solution)/shard_map/conv_finish/pallas_call | solution.py:35
  167.9 30.9 %all_to_all.32.recv_in_ref = bf16[32,64,256]{2,1,0:T(8,128)(2,1)} all-to-all(bf16[32,64,256]{2,1,0:T(8,128)(2,1)S(1)} %get-tuple-element.64), channel_id=1, replica_groups=mesh['gx'=2,'gy'=4,'gz'=4] {'gx','gz'}, dimensions={0} | all-to-all | bytes 2097152 | tf_op jit(solution)/shard_map/all_to_all | solution.py:838
  198.8 17.7 %owner_a.3 = (bf16[32,32,256]{2,1,0:T(8,128)(2,1)}, bf16[512,256]{1,0:T(8,128)(2,1)}, bf16[512,256]{1,0:T(8,128)(2,1)}, bf16[256,1024]{1,0:T(8,128)(2,1)}, bf16[1024,256]{1,0:T(8,128)(2,1)}, /*index=5*/s32[32]{0:T(128)}) custom-call(bf16[32,64,256]{2,1,0:T(8,128)(2,1)} %all_to_all.32.recv_in_ref, bf16[2,256,768]{2,1,0:T(8,128)(2,1)} %qkv_in_ref.3, ...), custom_call_target="tpu_custom_call" | custom-call | flops 8589934592 | bytes 1048576 | tf_op jit(solution)/shard_map/owner_a/pallas_call | solution.py:35
  216.5 3.5 %all-to-all-start.4 = ((bf16[32,32,256]{2,1,0:T(8,128)(2,1)}), bf16[32,32,256]{2,1,0:T(8,128)(2,1)S(1)}, u32[]{:S(2)}, u32[]{:S(2)}) async-start(bf16[32,32,256]{2,1,0:T(8,128)(2,1)} %get-tuple-element.65), calls=%async_computation.4 | async-start | bytes 1048576 | tf_op jit(solution)/shard_map/all_to_all | solution.py:840
  220.0 16.5 %owner_b.3 = bf16[32,32,256]{2,1,0:T(8,128)(2,1)} custom-call(s32[32]{0:T(128)} %get-tuple-element.66.pos_ref, bf16[512,256]{1,0:T(8,128)(2,1)} %get-tuple-element.67.x_in_ref, bf16[512,256]{1,0:T(8,128)(2,1)} %get-tuple-element.68.q_in_ref, bf16[256,1024]{1,0:T(8,128)(2,1)} %get-tuple-element.69.kt_in_ref, bf16[1024,256]{1,0:T(8,128)(2,1)} %get-tuple-element.70.v_in_ref, ...), custom_call_target="tpu_custom_call" | custom-call | flops 8589934592 | bytes 1048576 | tf_op jit(solution)/shard_map/owner_b/pallas_call | solution.py:35
  236.5 22.8 %all_to_all.33.back_b_ref = bf16[32,32,256]{2,1,0:T(8,128)(2,1)} all-to-all(bf16[32,32,256]{2,1,0:T(8,128)(2,1)} %owner_b.3), channel_id=1, replica_groups=mesh['gx'=2,'gy'=4,'gz'=4] {'gx','gz'}, dimensions={0} | all-to-all | bytes 1048576 | tf_op jit(solution)/shard_map/all_to_all | solution.py:840
  259.4 3.6 %restore.1 = f32[1920,256]{1,0:T(8,128)} custom-call(s32[1]{0:T(128)} %bitcast.18.count_ref, s32[30]{0:T(128)} %bitcast.47, bf16[46080,256]{1,0:T(8,128)(2,1)} %get-tuple-element.63.first_ref, bf16[32,32,256]{2,1,0:T(8,128)(2,1)} %copy-done.5, bf16[32,32,256]{2,1,0:T(8,128)(2,1)} %all_to_all.33.back_b_ref), custom_call_target="tpu_custom_call" | custom-call | tf_op jit(solution)/shard_map/restore/pallas_call | solution.py:35
  (14 shorter events, 0.0 us)
Async XLA Ops:
  0.7 1.5 copy-start
  2.3 0.7 copy-start.1
  8.0 7.1 %collective-permute-start = (bf16[1,8,16,256]{3,2,1,0:T(8,128)(2,1)S(1)}, bf16[1,8,16,256]{3,2,1,0:T(8,128)(2,1)S(1)}, u32[]{:S(2)}, u32[]{:S(2)}) collective-permute-start(bf16[1,8,16,256]{3,2,1,0:T(8,128)(2,1)S(1)} %bitcast.52), channel_id=1, source_target_pairs={{0,16},{16,0},{1,17},{17,1},{2,18},{18,2},{3,19},{19,3},{4,20},{20... | collective-permute-start | bytes 196616 | tf_op jit(solution)/shard_map/ppermute | solution.py:688
  15.7 9.4 %collective-permute-start.1 = (bf16[18,16,256]{2,1,0:T(8,128)(2,1)S(1)}, bf16[18,16,256]{2,1,0:T(8,128)(2,1)S(1)}, u32[]{:S(2)}, u32[]{:S(2)}) collective-permute-start(bf16[18,16,256]{2,1,0:T(8,128)(2,1)S(1)} %get-tuple-element.41), channel_id=1, source_target_pairs={{0,1},{1,2},{2,3},{4,5},{5,6},{6,7},{8,9},{9,10},{10,11},{12,13},{... | collective-permute-start | bytes 442376 | tf_op jit(solution)/shard_map/ppermute | solution.py:681
  19.2 7.0 %collective-permute-start.2 = (bf16[18,16,256]{2,1,0:T(8,128)(2,1)S(1)}, bf16[18,16,256]{2,1,0:T(8,128)(2,1)S(1)}, u32[]{:S(2)}, u32[]{:S(2)}) collective-permute-start(bf16[18,16,256]{2,1,0:T(8,128)(2,1)S(1)} %get-tuple-element.42), channel_id=1, source_target_pairs={{1,0},{2,1},{3,2},{5,4},{6,5},{7,6},{9,8},{10,9},{11,10},{13,12},{... | collective-permute-start | bytes 442376 | tf_op jit(solution)/shard_map/ppermute | solution.py:682
  27.3 6.7 %collective-permute-start.3 = (bf16[288,256]{1,0:T(8,128)(2,1)S(1)}, bf16[288,256]{1,0:T(8,128)(2,1)S(1)}, u32[]{:S(2)}, u32[]{:S(2)}) collective-permute-start(bf16[288,256]{1,0:T(8,128)(2,1)S(1)} %get-tuple-element.44), channel_id=1, source_target_pairs={{0,4},{4,8},{8,12},{1,5},{5,9},{9,13},{2,6},{6,10},{10,14},{3,7},{... | collective-permute-start | bytes 442376 | tf_op jit(solution)/shard_map/ppermute | solution.py:681
  28.6 5.4 %collective-permute-start.4 = (bf16[288,256]{1,0:T(8,128)(2,1)S(1)}, bf16[288,256]{1,0:T(8,128)(2,1)S(1)}, u32[]{:S(2)}, u32[]{:S(2)}) collective-permute-start(bf16[288,256]{1,0:T(8,128)(2,1)S(1)} %get-tuple-element.45), channel_id=1, source_target_pairs={{4,0},{8,4},{12,8},{5,1},{9,5},{13,9},{6,2},{10,6},{14,10},{7,3},{... | collective-permute-start | bytes 442376 | tf_op jit(solution)/shard_map/ppermute | solution.py:682
  30.7 3.3 %copy-start.4 = (s32[1,1,1,15]{3,2,1,0:T(1,128)S(1)}, s32[1,1,1,15]{3,2,1,0:T(1,128)}, u32[]{:S(2)}) copy-start(s32[1,1,1,15]{3,2,1,0:T(1,128)} %param.13) | copy-start | bytes 184
  92.1 20.3 %all-to-all-start.1 = ((bf16[16,64,256]{2,1,0:T(8,128)(2,1)}), bf16[16,64,256]{2,1,0:T(8,128)(2,1)S(1)}, u32[]{:S(2)}, u32[]{:S(2)}) async-start(bf16[16,64,256]{2,1,0:T(8,128)(2,1)} %get-tuple-element.48), calls=%async_computation.1 | async-start | bytes 1048576 | tf_op jit(solution)/shard_map/all_to_all | solution.py:840
  95.9 37.9 %copy-start.2 = (s32[1,1,1,1920]{3,2,1,0:T(1,128)S(1)}, s32[1,1,1,1920]{3,2,1,0:T(1,128)}, u32[]{:S(2)}) copy-start(s32[1,1,1,1920]{3,2,1,0:T(1,128)} %param.11) | copy-start | bytes 23044
  140.9 4.6 %collective-permute-start.5 = (bf16[1,8,16,256]{3,2,1,0:T(8,128)(2,1)S(1)}, bf16[1,8,16,256]{3,2,1,0:T(8,128)(2,1)S(1)}, u32[]{:S(2)}, u32[]{:S(2)}) collective-permute-start(bf16[1,8,16,256]{3,2,1,0:T(8,128)(2,1)S(1)} %bitcast.51), channel_id=1, source_target_pairs={{0,16},{16,0},{1,17},{17,1},{2,18},{18,2},{3,19},{19,3},{4,20},{20... | collective-permute-start | bytes 196616 | tf_op jit(solution)/shard_map/ppermute | solution.py:688
  146.0 7.7 %collective-permute-start.6 = (bf16[18,16,256]{2,1,0:T(8,128)(2,1)S(1)}, bf16[18,16,256]{2,1,0:T(8,128)(2,1)S(1)}, u32[]{:S(2)}, u32[]{:S(2)}) collective-permute-start(bf16[18,16,256]{2,1,0:T(8,128)(2,1)S(1)} %get-tuple-element.57), channel_id=1, source_target_pairs={{0,1},{1,2},{2,3},{4,5},{5,6},{6,7},{8,9},{9,10},{10,11},{12,13},{... | collective-permute-start | bytes 442376 | tf_op jit(solution)/shard_map/ppermute | solution.py:681
  147.8 7.3 %collective-permute-start.7 = (bf16[18,16,256]{2,1,0:T(8,128)(2,1)S(1)}, bf16[18,16,256]{2,1,0:T(8,128)(2,1)S(1)}, u32[]{:S(2)}, u32[]{:S(2)}) collective-permute-start(bf16[18,16,256]{2,1,0:T(8,128)(2,1)S(1)} %get-tuple-element.58), channel_id=1, source_target_pairs={{1,0},{2,1},{3,2},{5,4},{6,5},{7,6},{9,8},{10,9},{11,10},{13,12},{... | collective-permute-start | bytes 442376 | tf_op jit(solution)/shard_map/ppermute | solution.py:682
  156.2 6.7 %collective-permute-start.8 = (bf16[288,256]{1,0:T(8,128)(2,1)S(1)}, bf16[288,256]{1,0:T(8,128)(2,1)S(1)}, u32[]{:S(2)}, u32[]{:S(2)}) collective-permute-start(bf16[288,256]{1,0:T(8,128)(2,1)S(1)} %get-tuple-element.60), channel_id=1, source_target_pairs={{0,4},{4,8},{8,12},{1,5},{5,9},{9,13},{2,6},{6,10},{10,14},{3,7},{... | collective-permute-start | bytes 442376 | tf_op jit(solution)/shard_map/ppermute | solution.py:681
  157.5 5.4 %collective-permute-start.9 = (bf16[288,256]{1,0:T(8,128)(2,1)S(1)}, bf16[288,256]{1,0:T(8,128)(2,1)S(1)}, u32[]{:S(2)}, u32[]{:S(2)}) collective-permute-start(bf16[288,256]{1,0:T(8,128)(2,1)S(1)} %get-tuple-element.61), channel_id=1, source_target_pairs={{4,0},{8,4},{12,8},{5,1},{9,5},{13,9},{6,2},{10,6},{14,10},{7,3},{... | collective-permute-start | bytes 442376 | tf_op jit(solution)/shard_map/ppermute | solution.py:682
  159.6 3.3 %copy-start.3 = (s32[1,1,1,30]{3,2,1,0:T(1,128)S(1)}, s32[1,1,1,30]{3,2,1,0:T(1,128)}, u32[]{:S(2)}) copy-start(s32[1,1,1,30]{3,2,1,0:T(1,128)} %param.14) | copy-start | bytes 364
  216.5 20.0 %all-to-all-start.4 = ((bf16[32,32,256]{2,1,0:T(8,128)(2,1)}), bf16[32,32,256]{2,1,0:T(8,128)(2,1)S(1)}, u32[]{:S(2)}, u32[]{:S(2)}) async-start(bf16[32,32,256]{2,1,0:T(8,128)(2,1)} %get-tuple-element.65), calls=%async_computation.4 | async-start | bytes 1048576 | tf_op jit(solution)/shard_map/all_to_all | solution.py:840
  236.5 22.8 %copy-start.5 = (bf16[32,32,256]{2,1,0:T(8,128)(2,1)}, bf16[32,32,256]{2,1,0:T(8,128)(2,1)S(1)}, u32[]{:S(2)}) copy-start(bf16[32,32,256]{2,1,0:T(8,128)(2,1)S(1)} %all-to-all-done.4.back_a_ref) | copy-start | bytes 1572868

commit v3 on v2

--- a/solution.py
+++ b/solution.py
@@ -453,12 +453,13 @@
         pltpu.make_async_copy(first_vmem.at[rows], first_ref.at[rows], fsems.at[g]).wait()
 
 
-def attend_and_feed(x_ref, q_ref, kt_ref, va_ref, vb_ref, proj_ref, up_ref, down_ref, heads_ref, s0_ref, s1_ref, delta_ref, awaited):
+def attend_and_feed(x_ref, q_ref, kt_ref, v_ref, proj_ref, up_ref, down_ref, heads_ref, s0_ref, s1_ref, delta_ref, awaited):
     tile, channels = q_ref.shape
     half = channels // 2
     width = channels // HEADS
     scale = math.log2(math.e) / math.sqrt(width)
     group = iota((tile, half), 1) // width
+    ones = jnp.ones((PATCH, half), BF16)
 
     def score(h, side):
         cols = slice(side * half, (side + 1) * half)
@@ -467,10 +468,10 @@
 
     def combine(h, side, scores):
         cols = slice(side * half, (side + 1) * half)
-        v_ref = (va_ref, vb_ref)[side]
+        rhs = jnp.concatenate([v_ref[:, cols], ones], axis=1)
         top = jnp.max(scores, axis=-1, keepdims=True)
         probs = jnp.exp2(((scores - top) * scale).astype(BF16))
-        res = jnp.dot(probs, v_ref[...], preferred_element_type=F32)
+        res = jnp.dot(probs, rhs, preferred_element_type=F32)
         heads_ref[:, cols] = jnp.where(group == h, res[:, :half] / res[:, half:], heads_ref[:, cols])
 
     s0_ref[...] = score(0, 0)
@@ -491,15 +492,6 @@
     hidden = jnp.dot(normed, up_ref[...], preferred_element_type=F32)
     hidden = (0.5 * hidden * (1.0 + lax.erf(hidden * (1.0 / math.sqrt(2.0))))).astype(BF16)
     delta_ref[...] = (update + jnp.dot(hidden, down_ref[...], preferred_element_type=F32)).astype(BF16)
-
-
-def with_ones(v_ref, va_ref, vb_ref):
-    rows, channels = v_ref.shape
-    half = channels // 2
-    ones = jnp.ones((rows, half), BF16)
-    for side, ref in ((0, va_ref), (1, vb_ref)):
-        ref[:, :half] = v_ref[:, side * half : (side + 1) * half]
-        ref[:, half:] = ones
 
 
 def answer_copies(pos_ref, delta_ref, out_ref, sems):
@@ -531,8 +523,6 @@
     qb_ref,
     kt_ref,
     v_ref,
-    va_ref,
-    vb_ref,
     heads_ref,
     delta_ref,
     s0_ref,
@@ -580,9 +570,8 @@
     handed = [pltpu.make_async_copy(src, dst, sems.at[k]) for k, (src, dst) in enumerate(pairs)]
     for copy in handed:
         copy.start()
-    with_ones(v_ref, va_ref, vb_ref)
     attend_and_feed(
-        xa_ref, qa_ref, kt_ref, va_ref, vb_ref, proj_ref, up_ref, down_ref, heads_ref, s0_ref, s1_ref, delta_ref, weights[1:]
+        xa_ref, qa_ref, kt_ref, v_ref, proj_ref, up_ref, down_ref, heads_ref, s0_ref, s1_ref, delta_ref, weights[1:]
     )
     for copy in handed + answer_copies(pos_ref, delta_ref, out_ref, osems):
         copy.wait()
@@ -603,8 +592,6 @@
     q_ref,
     kt_ref,
     v_ref,
-    va_ref,
-    vb_ref,
     heads_ref,
     delta_ref,
     s0_ref,
@@ -624,10 +611,9 @@
         copy.start()
     for copy in copies[:3]:
         copy.wait()
-    with_ones(v_ref, va_ref, vb_ref)
     awaited = copies[3:] + weights
     attend_and_feed(
-        x_ref, q_ref, kt_ref, va_ref, vb_ref, proj_ref, up_ref, down_ref, heads_ref, s0_ref, s1_ref, delta_ref, awaited
+        x_ref, q_ref, kt_ref, v_ref, proj_ref, up_ref, down_ref, heads_ref, s0_ref, s1_ref, delta_ref, awaited
     )
     for copy in answer_copies(pos_ref, delta_ref, out_ref, osems):
         copy.wait()
@@ -645,7 +631,7 @@
     across = pltpu.VMEM((channels, PATCH), BF16)
     held = pltpu.VMEM((tile + part, channels), BF16)
     scores = pltpu.VMEM((tile, PATCH), F32)
-    tail = [across, whole, whole, whole, pltpu.VMEM((tile, channels), F32), half, scores, scores]
+    tail = [across, whole, pltpu.VMEM((tile, channels), F32), half, scores, scores]
     tail += [pltpu.SemaphoreType.DMA((4,)), pltpu.SemaphoreType.DMA((slots,))]
     answer = (sds((slots, part, channels), BF16), "h")
     rows = (sds((tile, channels), BF16), "h")

time: 264 us -> 263 us (level)
  no operation moved by 1% of the time
where the time goes in v3:
time: 263 us; the launch traced here: 262 us
  Pallas kernels  122 us (46%)
  blocking collectives  110 us (42%)
  starting transfers between devices  24 us (9%)
    pallas_call x21, Pallas kernels, call(): pl.pallas_call(kernel, out_shape=tuple((shape for shape, _ in outs)), gri...  122 us
    all_to_all x2, blocking collectives, body(): lax.all_to_all(send, axes[layer], split_axis=0, concat_axis=0, tiled=True)  66.2 us
    all_to_all x2, blocking collectives, body(): lax.all_to_all(a, axes[layer], split_axis=0, concat_axis=0, tiled=True)  44.2 us
    ppermute x4, starting transfers between devices, up_down(): lax.ppermute(high_face, axis, [(i, (i + 1) % count) for i in range(ends)])  7.88 us
    all_to_all x2, starting transfers between devices, body(): lax.all_to_all(a, axes[layer], split_axis=0, concat_axis=0, tiled=True)  7.27 us
  transfers between devices with their start and end apart: 12, of which 2 were waited for; matrix products, arithmetic and copies ran while one was open for 0% of the time, Pallas kernels for 22%

profile of v3, /device:TPU:0, one launch (start us, length us, event | category | flops | bytes accessed | tf_op | source)
XLA Modules:
  0.0 261.9 jit_solution(13933133120749091989)
XLA Ops:
  0.7 0.1 add_convert_fusion.flags_ref
  0.7 1.5 copy-done
  2.3 0.7 copy-done.1
  3.0 5.1 %place0.1 = (bf16[2048,256]{1,0:T(8,128)(2,1)S(1)}, bf16[1,128,256]{2,1,0:T(8,128)(2,1)S(1)}, bf16[2,288,256]{2,1,0:T(8,128)(2,1)S(1)}, bf16[27,256,256]{2,1,0:T(8,128)(2,1)S(1)}) custom-call(s32[2]{0:T(128)S(1)} %add_convert_fusion.flags_ref, s32[1]{0:T(128)} %bitcast.14.count_ref, s32[15,1,128]{2,1,0:T(1,128)S(1)} %bitcast.41, f32[1920,256]{1,0:T(8,128)S(1)} %bitcast.19, ...), custom_call_target="tpu_custom_call" | custom-call | tf_op jit(solution)/shard_map/place0/pallas_call | solution.py:35
  8.0 3.1 %collective-permute-start = (bf16[1,8,16,256]{3,2,1,0:T(8,128)(2,1)S(1)}, bf16[1,8,16,256]{3,2,1,0:T(8,128)(2,1)S(1)}, u32[]{:S(2)}, u32[]{:S(2)}) collective-permute-start(bf16[1,8,16,256]{3,2,1,0:T(8,128)(2,1)S(1)} %bitcast.52), channel_id=1, source_target_pairs={{0,16},{16,0},{1,17},{17,1},{2,18},{18,2},{3,19},{19,3},{4,20},{20... | collective-permute-start | bytes 196616 | tf_op jit(solution)/shard_map/ppermute | solution.py:674
  11.1 4.0 %conv_middle.2.after_ref.middle_ref = bf16[1024,256]{1,0:T(8,128)(2,1)S(1)} custom-call(bf16[16,8,16,256]{3,2,1,0:T(8,128)(2,1)S(1)} %bitcast.25, bf16[27,256,256]{2,1,0:T(8,128)(2,1)S(1)} %get-tuple-element.39.w_ref), custom_call_target="tpu_custom_call" | custom-call | flops 3623878656 | bytes 1048576 | tf_op jit(solution)/shard_map/conv_middle/pallas_call | solution.py:35
  15.1 0.0 collective-permute-done
  15.2 0.6 zface.2
  15.7 3.5 %collective-permute-start.1 = (bf16[18,16,256]{2,1,0:T(8,128)(2,1)S(1)}, bf16[18,16,256]{2,1,0:T(8,128)(2,1)S(1)}, u32[]{:S(2)}, u32[]{:S(2)}) collective-permute-start(bf16[18,16,256]{2,1,0:T(8,128)(2,1)S(1)} %get-tuple-element.41), channel_id=1, source_target_pairs={{0,1},{1,2},{2,3},{4,5},{5,6},{6,7},{8,9},{9,10},{10,11},{12,13},{... | collective-permute-start | bytes 442376 | tf_op jit(solution)/shard_map/ppermute | solution.py:667
  19.2 1.3 collective-permute-start.2
  20.5 4.6 %conv_ends.2.ends_ref.after_ref = bf16[1024,256]{1,0:T(8,128)(2,1)S(1)} custom-call(s32[2]{0:T(128)S(1)} %add_convert_fusion.flags_ref, bf16[16,8,16,256]{3,2,1,0:T(8,128)(2,1)S(1)} %bitcast.28, bf16[8,16,256]{2,1,0:T(8,128)(2,1)S(1)} %bitcast.31, bf16[8,16,256]{2,1,0:T(8,128)(2,1)S(1)} %bitcast.32, bf16[27,256,256]{2,1,0:T(8,128)(2,1)S(1)} %get-tuple-element.39.w_ref), custom_call_target="tpu_custom_call" | custom-call | flops 3623878656 | bytes 1048576 | tf_op jit(solution)/shard_map/conv_ends/pallas_call | solution.py:35
  25.1 1.1 collective-permute-done.2.zhi_ref
  26.3 1.0 yface.2
  27.3 1.3 collective-permute-start.3
  28.6 1.3 collective-permute-start.4
  29.9 0.8 conv_z.2.zc_ref
  30.7 0.0 copy-start.4
  30.7 3.3 %gather.2.main_ref = f32[1920,256]{1,0:T(8,128)S(1)} custom-call(s32[15,1,128]{2,1,0:T(1,128)S(1)} %bitcast.42, bf16[1024,256]{1,0:T(8,128)(2,1)S(1)} %conv_middle.2.after_ref.middle_ref, bf16[1024,256]{1,0:T(8,128)(2,1)S(1)} %conv_ends.2.ends_ref.after_ref, f32[2,16,16,256]{3,2,1,0:T(8,128)S(1)} %conv_z.2.zc_ref), custom_call_target="tpu_custom_call" | custom-call | flops 1811939328 | bytes 1048576 | tf_op jit(solution)/shard_map/gather/pallas_call | solution.py:35
  34.0 0.0 collective-permute-done.3.lo_ref
  34.0 5.0 %conv_finish.2 = (bf16[46080,256]{1,0:T(8,128)(2,1)}, bf16[16,128,256]{2,1,0:T(8,128)(2,1)S(1)}) custom-call(s32[1]{0:T(128)} %bitcast.15.count_ref, s32[15]{0:T(128)S(1)} %bitcast.49, s32[15,1,128]{2,1,0:T(1,128)S(1)} %bitcast.43, f32[1920,256]{1,0:T(8,128)S(1)} %gather.2.main_ref, bf16[288,256]{1,0:T(8,128)(2,1)S(1)} %collective-permute-done.3.lo_ref, ...), custom_call_target="tpu_custom_call" | custom-call | tf_op jit(solution)/shard_map/conv_finish/pallas_call | solution.py:35
  39.0 35.6 %all_to_all.30.recv_in_ref = bf16[16,128,256]{2,1,0:T(8,128)(2,1)} all-to-all(bf16[16,128,256]{2,1,0:T(8,128)(2,1)S(1)} %get-tuple-element.47), channel_id=1, replica_groups=mesh['gx'=2,'gy'=4,'gz'=4] {'gy','gz'}, dimensions={0} | all-to-all | bytes 2097152 | tf_op jit(solution)/shard_map/all_to_all | solution.py:824
  74.6 17.2 %owner_a.2 = (bf16[16,64,256]{2,1,0:T(8,128)(2,1)}, bf16[512,256]{1,0:T(8,128)(2,1)}, bf16[512,256]{1,0:T(8,128)(2,1)}, bf16[256,1024]{1,0:T(8,128)(2,1)}, bf16[1024,256]{1,0:T(8,128)(2,1)}, /*index=5*/s32[16]{0:T(128)}) custom-call(bf16[16,128,256]{2,1,0:T(8,128)(2,1)} %all_to_all.30.recv_in_ref, bf16[2,256,768]{2,1,0:T(8,128)(2,1)} %qkv_in_ref.3, ...), custom_call_target="tpu_custom_call" | custom-call | flops 8589934592 | bytes 1048576 | tf_op jit(solution)/shard_map/owner_a/pallas_call | solution.py:35
  91.8 3.8 %all-to-all-start.1 = ((bf16[16,64,256]{2,1,0:T(8,128)(2,1)}), bf16[16,64,256]{2,1,0:T(8,128)(2,1)S(1)}, u32[]{:S(2)}, u32[]{:S(2)}) async-start(bf16[16,64,256]{2,1,0:T(8,128)(2,1)} %get-tuple-element.48), calls=%async_computation.1 | async-start | bytes 1048576 | tf_op jit(solution)/shard_map/all_to_all | solution.py:826
  95.6 0.0 copy-start.2
  95.6 16.3 %owner_b.2 = bf16[16,64,256]{2,1,0:T(8,128)(2,1)} custom-call(s32[16]{0:T(128)} %get-tuple-element.49.pos_ref, bf16[512,256]{1,0:T(8,128)(2,1)} %get-tuple-element.50.x_in_ref, bf16[512,256]{1,0:T(8,128)(2,1)} %get-tuple-element.51.q_in_ref, bf16[256,1024]{1,0:T(8,128)(2,1)} %get-tuple-element.52.kt_in_ref, bf16[1024,256]{1,0:T(8,128)(2,1)} %get-tuple-element.53.v_in_ref, ...), custom_call_target="tpu_custom_call" | custom-call | flops 8589934592 | bytes 1048576 | tf_op jit(solution)/shard_map/owner_b/pallas_call | solution.py:35
  111.9 0.0 all-to-all-done.1.back_a_ref
  111.9 21.3 %all_to_all.31.back_b_ref = bf16[16,64,256]{2,1,0:T(8,128)(2,1)S(1)} all-to-all(bf16[16,64,256]{2,1,0:T(8,128)(2,1)} %owner_b.2), channel_id=1, replica_groups=mesh['gx'=2,'gy'=4,'gz'=4] {'gy','gz'}, dimensions={0} | all-to-all | bytes 1048576 | tf_op jit(solution)/shard_map/all_to_all | solution.py:826
  133.3 7.1 %place1.1 = (bf16[2048,256]{1,0:T(8,128)(2,1)S(1)}, bf16[1,128,256]{2,1,0:T(8,128)(2,1)S(1)}, bf16[2,288,256]{2,1,0:T(8,128)(2,1)S(1)}, bf16[27,256,256]{2,1,0:T(8,128)(2,1)S(1)}, f32[1920,256]{1,0:T(8,128)S(1)}) custom-call(s32[2]{0:T(128)S(1)} %add_convert_fusion.flags_ref, s32[1]{0:T(128)} %bitcast.16.count_ref, s32[15]{0:T(128)S(1)} %bitcast.50, ...), custom_call_target="tpu_custom_call" | custom-call | tf_op jit(solution)/shard_map/place1/pallas_call | solution.py:35
  140.4 0.6 collective-permute-start.5
  140.9 4.0 %conv_middle.3.after_ref.middle_ref = bf16[1024,256]{1,0:T(8,128)(2,1)S(1)} custom-call(bf16[16,8,16,256]{3,2,1,0:T(8,128)(2,1)S(1)} %bitcast.21, bf16[27,256,256]{2,1,0:T(8,128)(2,1)S(1)} %get-tuple-element.55.w_ref), custom_call_target="tpu_custom_call" | custom-call | flops 3623878656 | bytes 1048576 | tf_op jit(solution)/shard_map/conv_middle/pallas_call | solution.py:35
  145.0 0.6 zface.3
  145.6 1.8 collective-permute-start.6
  147.4 1.3 collective-permute-start.7
  148.7 4.6 %conv_ends.3.ends_ref.after_ref = bf16[1024,256]{1,0:T(8,128)(2,1)S(1)} custom-call(s32[2]{0:T(128)S(1)} %add_convert_fusion.flags_ref, bf16[16,8,16,256]{3,2,1,0:T(8,128)(2,1)S(1)} %bitcast.24, bf16[8,16,256]{2,1,0:T(8,128)(2,1)S(1)} %bitcast.37, bf16[8,16,256]{2,1,0:T(8,128)(2,1)S(1)} %bitcast.38, bf16[27,256,256]{2,1,0:T(8,128)(2,1)S(1)} %get-tuple-element.55.w_ref), custom_call_target="tpu_custom_call" | custom-call | flops 3623878656 | bytes 1048576 | tf_op jit(solution)/shard_map/conv_ends/pallas_call | solution.py:35
  153.3 1.4 collective-permute-done.7.zhi_ref
  154.7 1.0 yface.3
  155.7 1.3 collective-permute-start.8
  157.0 1.3 collective-permute-start.9
  158.3 0.8 conv_z.3.zc_ref
  159.1 0.0 copy-start.3
  159.1 3.2 %gather.3.main_ref = f32[1920,256]{1,0:T(8,128)S(1)} custom-call(s32[15,1,128]{2,1,0:T(1,128)S(1)} %bitcast.45, bf16[1024,256]{1,0:T(8,128)(2,1)S(1)} %conv_middle.3.after_ref.middle_ref, bf16[1024,256]{1,0:T(8,128)(2,1)S(1)} %conv_ends.3.ends_ref.after_ref, f32[2,16,16,256]{3,2,1,0:T(8,128)S(1)} %conv_z.3.zc_ref), custom_call_target="tpu_custom_call" | custom-call | flops 1811939328 | bytes 1048576 | tf_op jit(solution)/shard_map/gather/pallas_call | solution.py:35
  162.4 5.1 %conv_finish.3 = (bf16[46080,256]{1,0:T(8,128)(2,1)}, bf16[32,64,256]{2,1,0:T(8,128)(2,1)S(1)}) custom-call(s32[1]{0:T(128)} %bitcast.17.count_ref, s32[30]{0:T(128)S(1)} %bitcast.48, s32[15,1,128]{2,1,0:T(1,128)S(1)} %bitcast.46, f32[1920,256]{1,0:T(8,128)S(1)} %gather.3.main_ref, bf16[288,256]{1,0:T(8,128)(2,1)S(1)} %collective-permute-done.8.lo_ref, ...), custom_call_target="tpu_custom_call" | custom-call | tf_op jit(solution)/shard_map/conv_finish/pallas_call | solution.py:35
  167.5 30.6 %all_to_all.32.recv_in_ref = bf16[32,64,256]{2,1,0:T(8,128)(2,1)} all-to-all(bf16[32,64,256]{2,1,0:T(8,128)(2,1)S(1)} %get-tuple-element.64), channel_id=1, replica_groups=mesh['gx'=2,'gy'=4,'gz'=4] {'gx','gz'}, dimensions={0} | all-to-all | bytes 2097152 | tf_op jit(solution)/shard_map/all_to_all | solution.py:824
  198.1 17.4 %owner_a.3 = (bf16[32,32,256]{2,1,0:T(8,128)(2,1)}, bf16[512,256]{1,0:T(8,128)(2,1)}, bf16[512,256]{1,0:T(8,128)(2,1)}, bf16[256,1024]{1,0:T(8,128)(2,1)}, bf16[1024,256]{1,0:T(8,128)(2,1)}, /*index=5*/s32[32]{0:T(128)}) custom-call(bf16[32,64,256]{2,1,0:T(8,128)(2,1)} %all_to_all.32.recv_in_ref, bf16[2,256,768]{2,1,0:T(8,128)(2,1)} %qkv_in_ref.3, ...), custom_call_target="tpu_custom_call" | custom-call | flops 8589934592 | bytes 1048576 | tf_op jit(solution)/shard_map/owner_a/pallas_call | solution.py:35
  215.5 3.5 %all-to-all-start.4 = ((bf16[32,32,256]{2,1,0:T(8,128)(2,1)}), bf16[32,32,256]{2,1,0:T(8,128)(2,1)S(1)}, u32[]{:S(2)}, u32[]{:S(2)}) async-start(bf16[32,32,256]{2,1,0:T(8,128)(2,1)} %get-tuple-element.65), calls=%async_computation.4 | async-start | bytes 1048576 | tf_op jit(solution)/shard_map/all_to_all | solution.py:826
  219.0 16.3 %owner_b.3 = bf16[32,32,256]{2,1,0:T(8,128)(2,1)} custom-call(s32[32]{0:T(128)} %get-tuple-element.66.pos_ref, bf16[512,256]{1,0:T(8,128)(2,1)} %get-tuple-element.67.x_in_ref, bf16[512,256]{1,0:T(8,128)(2,1)} %get-tuple-element.68.q_in_ref, bf16[256,1024]{1,0:T(8,128)(2,1)} %get-tuple-element.69.kt_in_ref, bf16[1024,256]{1,0:T(8,128)(2,1)} %get-tuple-element.70.v_in_ref, ...), custom_call_target="tpu_custom_call" | custom-call | flops 8589934592 | bytes 1048576 | tf_op jit(solution)/shard_map/owner_b/pallas_call | solution.py:35
  235.3 22.8 %all_to_all.33.back_b_ref = bf16[32,32,256]{2,1,0:T(8,128)(2,1)} all-to-all(bf16[32,32,256]{2,1,0:T(8,128)(2,1)} %owner_b.3), channel_id=1, replica_groups=mesh['gx'=2,'gy'=4,'gz'=4] {'gx','gz'}, dimensions={0} | all-to-all | bytes 1048576 | tf_op jit(solution)/shard_map/all_to_all | solution.py:826
  258.2 3.6 %restore.1 = f32[1920,256]{1,0:T(8,128)} custom-call(s32[1]{0:T(128)} %bitcast.18.count_ref, s32[30]{0:T(128)} %bitcast.47, bf16[46080,256]{1,0:T(8,128)(2,1)} %get-tuple-element.63.first_ref, bf16[32,32,256]{2,1,0:T(8,128)(2,1)} %copy-done.5, bf16[32,32,256]{2,1,0:T(8,128)(2,1)} %all_to_all.33.back_b_ref), custom_call_target="tpu_custom_call" | custom-call | tf_op jit(solution)/shard_map/restore/pallas_call | solution.py:35
  (14 shorter events, 0.0 us)
Async XLA Ops:
  0.7 1.5 copy-start
  2.3 0.7 copy-start.1
  8.0 7.1 %collective-permute-start = (bf16[1,8,16,256]{3,2,1,0:T(8,128)(2,1)S(1)}, bf16[1,8,16,256]{3,2,1,0:T(8,128)(2,1)S(1)}, u32[]{:S(2)}, u32[]{:S(2)}) collective-permute-start(bf16[1,8,16,256]{3,2,1,0:T(8,128)(2,1)S(1)} %bitcast.52), channel_id=1, source_target_pairs={{0,16},{16,0},{1,17},{17,1},{2,18},{18,2},{3,19},{19,3},{4,20},{20... | collective-permute-start | bytes 196616 | tf_op jit(solution)/shard_map/ppermute | solution.py:674
  15.7 9.4 %collective-permute-start.1 = (bf16[18,16,256]{2,1,0:T(8,128)(2,1)S(1)}, bf16[18,16,256]{2,1,0:T(8,128)(2,1)S(1)}, u32[]{:S(2)}, u32[]{:S(2)}) collective-permute-start(bf16[18,16,256]{2,1,0:T(8,128)(2,1)S(1)} %get-tuple-element.41), channel_id=1, source_target_pairs={{0,1},{1,2},{2,3},{4,5},{5,6},{6,7},{8,9},{9,10},{10,11},{12,13},{... | collective-permute-start | bytes 442376 | tf_op jit(solution)/shard_map/ppermute | solution.py:667
  19.2 7.0 %collective-permute-start.2 = (bf16[18,16,256]{2,1,0:T(8,128)(2,1)S(1)}, bf16[18,16,256]{2,1,0:T(8,128)(2,1)S(1)}, u32[]{:S(2)}, u32[]{:S(2)}) collective-permute-start(bf16[18,16,256]{2,1,0:T(8,128)(2,1)S(1)} %get-tuple-element.42), channel_id=1, source_target_pairs={{1,0},{2,1},{3,2},{5,4},{6,5},{7,6},{9,8},{10,9},{11,10},{13,12},{... | collective-permute-start | bytes 442376 | tf_op jit(solution)/shard_map/ppermute | solution.py:668
  27.3 6.7 %collective-permute-start.3 = (bf16[288,256]{1,0:T(8,128)(2,1)S(1)}, bf16[288,256]{1,0:T(8,128)(2,1)S(1)}, u32[]{:S(2)}, u32[]{:S(2)}) collective-permute-start(bf16[288,256]{1,0:T(8,128)(2,1)S(1)} %get-tuple-element.44), channel_id=1, source_target_pairs={{0,4},{4,8},{8,12},{1,5},{5,9},{9,13},{2,6},{6,10},{10,14},{3,7},{... | collective-permute-start | bytes 442376 | tf_op jit(solution)/shard_map/ppermute | solution.py:667
  28.6 5.4 %collective-permute-start.4 = (bf16[288,256]{1,0:T(8,128)(2,1)S(1)}, bf16[288,256]{1,0:T(8,128)(2,1)S(1)}, u32[]{:S(2)}, u32[]{:S(2)}) collective-permute-start(bf16[288,256]{1,0:T(8,128)(2,1)S(1)} %get-tuple-element.45), channel_id=1, source_target_pairs={{4,0},{8,4},{12,8},{5,1},{9,5},{13,9},{6,2},{10,6},{14,10},{7,3},{... | collective-permute-start | bytes 442376 | tf_op jit(solution)/shard_map/ppermute | solution.py:668
  30.7 3.3 %copy-start.4 = (s32[1,1,1,15]{3,2,1,0:T(1,128)S(1)}, s32[1,1,1,15]{3,2,1,0:T(1,128)}, u32[]{:S(2)}) copy-start(s32[1,1,1,15]{3,2,1,0:T(1,128)} %param.13) | copy-start | bytes 184
  91.8 20.1 %all-to-all-start.1 = ((bf16[16,64,256]{2,1,0:T(8,128)(2,1)}), bf16[16,64,256]{2,1,0:T(8,128)(2,1)S(1)}, u32[]{:S(2)}, u32[]{:S(2)}) async-start(bf16[16,64,256]{2,1,0:T(8,128)(2,1)} %get-tuple-element.48), calls=%async_computation.1 | async-start | bytes 1048576 | tf_op jit(solution)/shard_map/all_to_all | solution.py:826
  95.6 37.7 %copy-start.2 = (s32[1,1,1,1920]{3,2,1,0:T(1,128)S(1)}, s32[1,1,1,1920]{3,2,1,0:T(1,128)}, u32[]{:S(2)}) copy-start(s32[1,1,1,1920]{3,2,1,0:T(1,128)} %param.11) | copy-start | bytes 23044
  140.4 4.6 %collective-permute-start.5 = (bf16[1,8,16,256]{3,2,1,0:T(8,128)(2,1)S(1)}, bf16[1,8,16,256]{3,2,1,0:T(8,128)(2,1)S(1)}, u32[]{:S(2)}, u32[]{:S(2)}) collective-permute-start(bf16[1,8,16,256]{3,2,1,0:T(8,128)(2,1)S(1)} %bitcast.51), channel_id=1, source_target_pairs={{0,16},{16,0},{1,17},{17,1},{2,18},{18,2},{3,19},{19,3},{4,20},{20... | collective-permute-start | bytes 196616 | tf_op jit(solution)/shard_map/ppermute | solution.py:674
  145.6 7.7 %collective-permute-start.6 = (bf16[18,16,256]{2,1,0:T(8,128)(2,1)S(1)}, bf16[18,16,256]{2,1,0:T(8,128)(2,1)S(1)}, u32[]{:S(2)}, u32[]{:S(2)}) collective-permute-start(bf16[18,16,256]{2,1,0:T(8,128)(2,1)S(1)} %get-tuple-element.57), channel_id=1, source_target_pairs={{0,1},{1,2},{2,3},{4,5},{5,6},{6,7},{8,9},{9,10},{10,11},{12,13},{... | collective-permute-start | bytes 442376 | tf_op jit(solution)/shard_map/ppermute | solution.py:667
  147.4 7.3 %collective-permute-start.7 = (bf16[18,16,256]{2,1,0:T(8,128)(2,1)S(1)}, bf16[18,16,256]{2,1,0:T(8,128)(2,1)S(1)}, u32[]{:S(2)}, u32[]{:S(2)}) collective-permute-start(bf16[18,16,256]{2,1,0:T(8,128)(2,1)S(1)} %get-tuple-element.58), channel_id=1, source_target_pairs={{1,0},{2,1},{3,2},{5,4},{6,5},{7,6},{9,8},{10,9},{11,10},{13,12},{... | collective-permute-start | bytes 442376 | tf_op jit(solution)/shard_map/ppermute | solution.py:668
  155.7 6.7 %collective-permute-start.8 = (bf16[288,256]{1,0:T(8,128)(2,1)S(1)}, bf16[288,256]{1,0:T(8,128)(2,1)S(1)}, u32[]{:S(2)}, u32[]{:S(2)}) collective-permute-start(bf16[288,256]{1,0:T(8,128)(2,1)S(1)} %get-tuple-element.60), channel_id=1, source_target_pairs={{0,4},{4,8},{8,12},{1,5},{5,9},{9,13},{2,6},{6,10},{10,14},{3,7},{... | collective-permute-start | bytes 442376 | tf_op jit(solution)/shard_map/ppermute | solution.py:667
  157.0 5.4 %collective-permute-start.9 = (bf16[288,256]{1,0:T(8,128)(2,1)S(1)}, bf16[288,256]{1,0:T(8,128)(2,1)S(1)}, u32[]{:S(2)}, u32[]{:S(2)}) collective-permute-start(bf16[288,256]{1,0:T(8,128)(2,1)S(1)} %get-tuple-element.61), channel_id=1, source_target_pairs={{4,0},{8,4},{12,8},{5,1},{9,5},{13,9},{6,2},{10,6},{14,10},{7,3},{... | collective-permute-start | bytes 442376 | tf_op jit(solution)/shard_map/ppermute | solution.py:668
  159.1 3.3 %copy-start.3 = (s32[1,1,1,30]{3,2,1,0:T(1,128)S(1)}, s32[1,1,1,30]{3,2,1,0:T(1,128)}, u32[]{:S(2)}) copy-start(s32[1,1,1,30]{3,2,1,0:T(1,128)} %param.14) | copy-start | bytes 364
  215.5 19.8 %all-to-all-start.4 = ((bf16[32,32,256]{2,1,0:T(8,128)(2,1)}), bf16[32,32,256]{2,1,0:T(8,128)(2,1)S(1)}, u32[]{:S(2)}, u32[]{:S(2)}) async-start(bf16[32,32,256]{2,1,0:T(8,128)(2,1)} %get-tuple-element.65), calls=%async_computation.4 | async-start | bytes 1048576 | tf_op jit(solution)/shard_map/all_to_all | solution.py:826
  235.3 22.8 %copy-start.5 = (bf16[32,32,256]{2,1,0:T(8,128)(2,1)}, bf16[32,32,256]{2,1,0:T(8,128)(2,1)S(1)}, u32[]{:S(2)}) copy-start(bf16[32,32,256]{2,1,0:T(8,128)(2,1)S(1)} %all-to-all-done.4.back_a_ref) | copy-start | bytes 1572868
